TPU v7x, 256 devices: a whole 4x4x8 slice. The times are simulated.
256 devices in a mesh: area: 32 (over z, x), unit: 8 (over y, core).
Axes of the slice: x: 4, y: 4, z: 8, core: 2. Of those that a mesh axis runs over, the one named last changes fastest.
Arguments:
- initial_rates: float32 [32, 4096, 128], P('area', 'unit'), may hold values from -0.9 to 0.9
- prior_rates: bfloat16 [32, 4096, 128], P('area', 'unit'), may hold values from -0.8984375 to 0.8984375
- local_weight: bfloat16 [32, 4096, 4096], P('area', 'unit'), may hold values from -0.125 to 0.125
- long_weight: bfloat16 [32, 4096, 2048], P('area', 'unit'), may hold values from -0.1875 to 0.1875
- input_weight: bfloat16 [32, 4096, 16], P('area', 'unit'), may hold values from -1.5 to 1.5
- unit_bias: float32 [32, 4096], P('area', 'unit'), may hold values from -2.5 to 2.5
- leak_rate: float32 [32, 4096], P('area', 'unit'), may hold values from 0.2 to 1
- stimulus: bfloat16 [6, 16, 128], replicated, may hold values from -4 to 4
- link_source: int32 [32, 16], replicated, may hold values from 0 to 31, as said below
- link_block: int32 [32, 16], replicated, may hold values from 0 to 31
- link_delay: int32 [32, 16], replicated, may hold values from 0 to 1
Outputs:
- final_rates: float32 [32, 4096, 128], P('area', 'unit')
- final_current: float32 [32, 4096, 128], P('area', 'unit')
Inputs may be any that keep to these rules, and one draw needn't show every extreme that they name: `link_source`: each area's 16 entries name every source area at most 1 times, and some source area exactly 1 times.
All inputs are finite; a program needn't handle non-finite values.
Results may differ from a plain program's by a relative error of at most 0.004.
Values may be sent and summed in bfloat16 or wider, within the bound.
No kernel may reach another device: no remote copies, remote signals or barrier semaphores. Data moves between devices by JAX's collectives and lax.ppermute only.
A program may use at most 64 MiB of HBM per device.

v0:
```python
import jax
import jax.numpy as jnp
from jax import lax
from jax.experimental import pallas as pl
from jax.experimental.pallas import tpu as pltpu
from jax.sharding import PartitionSpec as P


UNITS = 4096
BLOCK = 128
WINDOWS = 3
ROWS = 512
HALF = BLOCK // 2
BLOCKS = UNITS // BLOCK


VMEM = pl.BlockSpec(memory_space=pltpu.VMEM)
SMEM = pl.BlockSpec(memory_space=pltpu.SMEM)
F32 = jnp.float32
BF16 = jnp.bfloat16

SRC, CORE, UNIT = 32, 48, 56


def put(pieces, first, full):
    for m, piece in enumerate(pieces):
        full[(first + m) * ROWS : (first + m + 1) * ROWS, :] = piece[...]


def put_own(table, piece, pair, full):
    other = pl.multiple_of((1 - table[CORE]) * ROWS, ROWS)
    full[0:ROWS, :] = piece[...]
    full[ROWS : 2 * ROWS, :] = pair[pl.ds(other, ROWS), :]


def by_rows(work):
    def one(i, carry):
        work(pl.ds(pl.multiple_of(i * (ROWS // 2), ROWS // 2), ROWS // 2))
        return carry

    lax.fori_loop(0, 2, one, 0)


def send(table, sources, outgoing):
    half = table[CORE] * HALF

    def one(area, carry):
        row = table[area]
        for array, first in sources:
            count = array.shape[0] // BLOCK

            @pl.when((row >= first) & (row < first + count))
            def _():
                start = pl.multiple_of((row - first) * BLOCK + half, HALF)
                outgoing[area] = array[pl.ds(start, HALF), :]

        return carry

    lax.fori_loop(0, BLOCKS, one, 0, unroll=4)


def product(table, weight, rows, full, first):
    total = None
    for m in range(full.shape[0] // ROWS):
        columns = pl.ds(pl.multiple_of(table[UNIT + first + m], ROWS), ROWS)
        part = jnp.dot(weight[rows, columns], full[m * ROWS : (m + 1) * ROWS, :], preferred_element_type=F32)
        total = part if total is None else total + part
    return total


def begin_kernel(table, piece, pair, near, near_other, earlier, front, outgoing):
    put_own(table, piece, pair, front)
    put((near, near_other), 2, front)
    send(table, ((front, 0), (earlier, BLOCKS)), outgoing)


def finish_kernel(table, *refs):
    *pieces, begun, back, outgoing = refs
    del begun
    put(pieces, 0, back)
    send(table, ((back, BLOCKS // 2),), outgoing)


def start_kernel(table, own, other, near, far, far_other, second, front, back, outgoing, earlier):
    mine = pl.multiple_of(table[CORE] * 2 * ROWS, 2 * ROWS)
    theirs = pl.multiple_of(2 * ROWS - mine, 2 * ROWS)
    for m, (piece, row) in enumerate(
        ((own, 0), (other, 0), (near, mine), (near, theirs), (far, 0), (far_other, 0), (second, mine), (second, theirs))
    ):
        full, first = (front, m * ROWS) if m < 4 else (back, (m - 4) * ROWS)
        full[first : first + ROWS, :] = piece[pl.ds(row, ROWS), :]
        earlier[m * ROWS : (m + 1) * ROWS, :] = piece[pl.ds(row + ROWS, ROWS), :]
    send(table, ((front, 0), (back, BLOCKS // 2), (earlier, BLOCKS)), outgoing)


def local_kernel(table, weight, front, back, drive, out):
    @by_rows
    def _(rows):
        total = product(table, weight, rows, front, 0) + product(table, weight, rows, back, 4)
        out[rows, :] = drive[rows, :] + total


def collect(table, mine, theirs, inputs):
    half = pl.multiple_of(table[CORE] * HALF, HALF)
    other = pl.multiple_of(HALF - half, HALF)
    for slot in range(16):
        area = table[SRC + slot]
        inputs[pl.ds(slot * BLOCK + half, HALF), :] = mine[area]
        inputs[pl.ds(slot * BLOCK + other, HALF), :] = theirs[area]


def current_kernel(table, weight, mine, theirs, current, inputs):
    collect(table, mine, theirs, inputs)

    @by_rows
    def _(rows):
        current[rows, :] = jnp.dot(weight[rows, :], inputs[...], preferred_element_type=F32)


def moved(rates, leak, drive):
    return rates + leak * (jnp.tanh(drive) - rates)


def first_kernel(table, weight, mine, theirs, partial, rates, leak, current, out, copy, inputs):
    collect(table, mine, theirs, inputs)

    @by_rows
    def _(rows):
        now = jnp.dot(weight[rows, :], inputs[...], preferred_element_type=F32)
        current[rows, :] = now
        new = moved(rates[rows, :], leak[rows, :], partial[rows, :] + now)
        out[rows, :] = new
        copy[rows, :] = new.astype(BF16)


def early_kernel(table, weight, piece, pair, *refs):
    *pieces, current, drive, out, full = refs
    put_own(table, piece, pair, full)
    put(pieces, 2, full)

    @by_rows
    def _(rows):
        total = product(table, weight, rows, full, 0)
        out[rows, :] = current[rows, :] + drive[rows, :] + total


def second_kernel(table, weight, *refs):
    *pieces, before, partial, rates, leak, full, out, copy = refs
    size = before.shape[0]
    full[0:size, :] = before[...]
    put(pieces, size // ROWS, full)

    @by_rows
    def _(rows):
        total = product(table, weight, rows, full.at[pl.ds(size, UNITS - size), :], size // ROWS)
        new = moved(rates[rows, :], leak[rows, :], partial[rows, :] + total)
        out[rows, :] = new
        copy[rows, :] = new.astype(BF16)


def drive_kernel(weight, stimulus, bias, leak, local_weight, out, leak_out):
    del local_weight
    leak_out[...] = leak[...]

    def one(n, carry):
        part = lax.dot_general(weight[...], stimulus[n], (((0,), (0,)), ((), ())), preferred_element_type=F32)
        out[n] = part + bias[...]
        return carry

    lax.fori_loop(0, 2 * WINDOWS, one, 0)


def both_kernel(rates, prior, out):
    out[0:ROWS, :] = rates[...].astype(BF16)
    out[ROWS : 2 * ROWS, :] = prior[...]


def call(kernel, inputs, outs, flops, scratch=(), aliases=None):
    byte_count = sum(x.size * x.dtype.itemsize for x in inputs)
    return pl.pallas_call(
        kernel,
        out_shape=outs,
        in_specs=[SMEM if x.dtype == jnp.int32 else VMEM for x in inputs],
        out_specs=jax.tree.map(lambda _: VMEM, outs),
        scratch_shapes=list(scratch),
        input_output_aliases=aliases or {},
        cost_estimate=pl.CostEstimate(flops=flops, bytes_accessed=byte_count, transcendentals=0),
        compiler_params=pltpu.CompilerParams(vmem_limit_bytes=24 * 2**20),
    )(*inputs)


def shape(rows, dtype):
    return jax.ShapeDtypeStruct((rows, BLOCK), dtype)


def paired(piece):
    return lax.all_gather(piece, "unit", axis=0, tiled=True, axis_index_groups=[[0, 1], [2, 3], [4, 5], [6, 7]])


PAIRS = [(u, u ^ 1) for u in range(8)]


def neighbours(piece):
    found = []
    for m in (2, 6, 4):
        found.append(lax.ppermute(piece, "unit", [(u, u ^ m) for u in range(8)]))
    return found


def exchange(piece):
    near, second, far = neighbours(piece)
    near, pair = lax.optimization_barrier((near, paired(piece)))
    pieces = [piece, pair]
    for x in (near, far, second):
        pieces += [x, lax.ppermute(x, "unit", PAIRS)]
    return pieces


def shards(
    initial_rates,
    prior_rates,
    local_weight,
    long_weight,
    input_weight,
    unit_bias,
    leak_rate,
    stimulus,
    link_source,
    link_block,
    link_delay,
):
    area_here = lax.axis_index("area")
    unit_here = lax.axis_index("unit")
    order = unit_here ^ jnp.arange(8, dtype=jnp.int32)
    place = link_block ^ (unit_here * (ROWS // BLOCK))
    block_row = link_delay * BLOCKS + place
    from_here = link_source == area_here
    send_rows = jnp.sum(jnp.where(from_here, block_row, 0), axis=1)
    own_source = lax.dynamic_index_in_dim(link_source, area_here, 0, keepdims=False)
    core = jnp.full((8,), unit_here % 2, jnp.int32)
    table = jnp.concatenate([send_rows, own_source, core, order * ROWS]).astype(jnp.int32)
    weight_local = local_weight[0]
    weight_long = long_weight[0]
    drives, leak = call(
        drive_kernel,
        [input_weight[0].T, stimulus, unit_bias[0][:, None], leak_rate[0][:, None], weight_local],
        (jax.ShapeDtypeStruct((2 * WINDOWS, ROWS, BLOCK), F32), jax.ShapeDtypeStruct((ROWS, 1), F32)),
        1000,
    )
    flops = ROWS * UNITS * BLOCK

    def long_range(outgoing):
        arrived = lax.all_to_all(outgoing, "area", split_axis=0, concat_axis=0, tiled=True)
        other = lax.ppermute(arrived, "unit", [(u, u ^ 1) for u in range(8)])
        return arrived, other

    gather_scratch = [pltpu.VMEM((16 * BLOCK, BLOCK), BF16)]
    history = shape(UNITS, BF16)
    parcels = jax.ShapeDtypeStruct((BLOCKS, HALF, BLOCK), BF16)
    half_history = shape(UNITS // 2, BF16)
    both = call(both_kernel, [initial_rates[0], prior_rates[0]], shape(2 * ROWS, BF16), 1000)
    near, second, far = neighbours(both)
    other = lax.ppermute(both, "unit", PAIRS)
    far, drives, leak = lax.optimization_barrier((far, drives, leak))
    pairs = [both, other, paired(near), far, lax.ppermute(far, "unit", PAIRS), paired(second)]
    *later, outgoing = call(
        start_kernel, [table, *pairs], (half_history, half_history, parcels), 1000, [pltpu.VMEM((UNITS, BLOCK), BF16)]
    )

    def window(step, carry):
        later, outgoing, rates = carry
        mine, theirs = long_range(outgoing)
        drive = [drives[2 * step + n] for n in range(2)]
        partial = call(local_kernel, [table, weight_local, *later, drive[0]], shape(ROWS, F32), 2 * flops)
        current, rates, copy = call(
            first_kernel,
            [table, weight_long, mine, theirs, partial, rates, leak],
            (shape(ROWS, F32), shape(ROWS, F32), shape(ROWS, BF16)),
            flops,
            gather_scratch,
        )
        pieces = exchange(copy)
        partial, before = call(
            early_kernel,
            [table, weight_local, *pieces[:4], current, drive[1]],
            (shape(ROWS, F32), shape(4 * ROWS, BF16)),
            flops,
        )
        earlier, rates, copy = call(
            second_kernel,
            [table, weight_local, *pieces[4:], before, partial, rates, leak],
            (history, shape(ROWS, F32), shape(ROWS, BF16)),
            flops,
        )
        pieces = exchange(copy)
        front, outgoing = call(begin_kernel, [table, *pieces[:4], earlier], (half_history, parcels), 1000)
        back, outgoing = call(
            finish_kernel, [table, *pieces[4:], outgoing], (half_history, parcels), 1000, aliases={5: 1}
        )
        later = [front, back]
        return later, outgoing, rates

    carry = (later, outgoing, initial_rates[0])
    for step in range(WINDOWS):
        carry = window(step, carry)
    later, outgoing, rates = carry
    mine, theirs = long_range(outgoing)
    final_current = call(current_kernel, [table, weight_long, mine, theirs], shape(ROWS, F32), flops, gather_scratch)
    return (rates[None], final_current[None])


def solution(mesh):
    return jax.shard_map(
        shards,
        mesh=mesh,
        in_specs=(
            P("area", "unit", None),
            P("area", "unit", None),
            P("area", "unit", None),
            P("area", "unit", None),
            P("area", "unit", None),
            P("area", "unit"),
            P("area", "unit"),
            P(),
            P(),
            P(),
            P(),
        ),
        out_specs=(P("area", "unit", None), P("area", "unit", None)),
        check_vma=False,
    )
```

profile of v0, /device:TPU:1, one launch (start us, length us, event | category | flops | bytes accessed | tf_op | source)
XLA Modules:
  0.0 216.9 jit_solution(5295378190694873588)
XLA Ops:
  2.5 3.6 %collective-permute-start.4 = (bf16[1024,128]{1,0:T(8,128)(2,1)S(1)}, bf16[1024,128]{1,0:T(8,128)(2,1)S(1)}, u32[]{:S(2)}, u32[]{:S(2)}) collective-permute-start(bf16[1024,128]{1,0:T(8,128)(2,1)S(1)} %shard_map.122.own), channel_id=1, source_target_pairs={{0,6},{1,7},{2,4},{3,5},{4,2},{5,3},{6,0},{7,1},{8,14},{9,15},{10,... | collective-permute-start | bytes 786440 | tf_op jit(solution)/shard_map/ppermute | solution.py:206
  6.8 3.1 %collective-permute-start = (bf16[1024,128]{1,0:T(8,128)(2,1)S(1)}, bf16[1024,128]{1,0:T(8,128)(2,1)S(1)}, u32[]{:S(2)}, u32[]{:S(2)}) collective-permute-start(bf16[1024,128]{1,0:T(8,128)(2,1)S(1)} %shard_map.122.own), channel_id=1, source_target_pairs={{0,1},{1,0},{2,3},{3,2},{4,5},{5,4},{6,7},{7,6},{8,9},{9,8},{10,11... | collective-permute-start | bytes 786440 | tf_op jit(solution)/shard_map/ppermute | solution.py:263
  12.3 2.2 %copy-done = bf16[1,512,4096]{2,1,0:T(8,128)(2,1)S(1)} copy-done((bf16[1,512,4096]{2,1,0:T(8,128)(2,1)S(1)}, bf16[1,512,4096]{2,1,0:T(8,128)(2,1)}, u32[]{:S(2)}) %copy-start) | copy-done | bytes 4194328
  17.9 3.0 %all_gather.25.second = bf16[2048,128]{1,0:T(8,128)(2,1)S(1)} all-gather(bf16[1024,128]{1,0:T(8,128)(2,1)S(1)} %collective-permute-done.4), channel_id=1, replica_groups={{0,1},{2,3},{4,5},{6,7},{8,9},{10,11},{12,13},{14,15},{16,17},{18,19},{..., dimensions={0}, use_global_device_ids=true | all-gather | bytes 786432 | tf_op jit(solution)/shard_map/all_gather | solution.py:197
  20.8 2.4 %all_gather.24.near = bf16[2048,128]{1,0:T(8,128)(2,1)S(1)} all-gather(bf16[1024,128]{1,0:T(8,128)(2,1)} %collective-permute-done.1), channel_id=1, replica_groups={{0,1},{2,3},{4,5},{6,7},{8,9},{10,11},{12,13},{14,15},{16,17},{18,19},{..., dimensions={0}, use_global_device_ids=true | all-gather | bytes 786432 | tf_op jit(solution)/shard_map/all_gather | solution.py:197
  24.6 27.7 %all_to_all.20.mine = bf16[32,64,128]{2,1,0:T(8,128)(2,1)S(1)} all-to-all(bf16[32,64,128]{2,1,0:T(8,128)(2,1)S(1)} %get-tuple-element.59), channel_id=1, replica_groups=mesh['area'=32,'unit'=8] {'area'}, dimensions={0} | all-to-all | bytes 1048576 | tf_op jit(solution)/shard_map/all_to_all | solution.py:253
  52.4 2.1 collective-permute-start.5
  54.6 1.9 shard_map.125.partial
  58.2 2.8 %collective-permute-start.8 = (bf16[512,128]{1,0:T(8,128)(2,1)S(1)}, bf16[512,128]{1,0:T(8,128)(2,1)S(1)}, u32[]{:S(2)}, u32[]{:S(2)}) collective-permute-start(bf16[512,128]{1,0:T(8,128)(2,1)S(1)} %get-tuple-element.64.piece), channel_id=1, source_target_pairs={{0,6},{1,7},{2,4},{3,5},{4,2},{5,3},{6,0},{7,1},{8,14},{9,15},{10,... | collective-permute-start | bytes 393224 | tf_op jit(solution)/shard_map/ppermute | solution.py:206
  62.1 2.2 %all_gather.26.pair = bf16[1024,128]{1,0:T(8,128)(2,1)S(1)} all-gather(bf16[512,128]{1,0:T(8,128)(2,1)S(1)} %get-tuple-element.64.piece), channel_id=1, replica_groups={{0,1},{2,3},{4,5},{6,7},{8,9},{10,11},{12,13},{14,15},{16,17},{18,19},{..., dimensions={0}, use_global_device_ids=true | all-gather | bytes 393216 | tf_op jit(solution)/shard_map/all_gather | solution.py:197
  64.6 1.9 collective-permute-done.8.refs_2_
  75.6 2.5 %all_gather.27.pair = bf16[1024,128]{1,0:T(8,128)(2,1)S(1)} all-gather(bf16[512,128]{1,0:T(8,128)(2,1)S(1)} %get-tuple-element.71.piece), channel_id=1, replica_groups={{0,1},{2,3},{4,5},{6,7},{8,9},{10,11},{12,13},{14,15},{16,17},{18,19},{..., dimensions={0}, use_global_device_ids=true | all-gather | bytes 393216 | tf_op jit(solution)/shard_map/all_gather | solution.py:197
  84.5 20.8 %all_to_all.21.mine = bf16[32,64,128]{2,1,0:T(8,128)(2,1)S(1)} all-to-all(bf16[32,64,128]{2,1,0:T(8,128)(2,1)S(1)} %get-tuple-element.76), channel_id=1, replica_groups=mesh['area'=32,'unit'=8] {'area'}, dimensions={0} | all-to-all | bytes 1048576 | tf_op jit(solution)/shard_map/all_to_all | solution.py:253
  105.2 2.1 collective-permute-start.18
  107.3 1.9 shard_map.131.partial
  114.1 2.5 %all_gather.28.pair = bf16[1024,128]{1,0:T(8,128)(2,1)S(1)} all-gather(bf16[512,128]{1,0:T(8,128)(2,1)S(1)} %get-tuple-element.80.piece), channel_id=1, replica_groups={{0,1},{2,3},{4,5},{6,7},{8,9},{10,11},{12,13},{14,15},{16,17},{18,19},{..., dimensions={0}, use_global_device_ids=true | all-gather | bytes 393216 | tf_op jit(solution)/shard_map/all_gather | solution.py:197
  117.3 2.2 %collective-permute-start.22 = (bf16[512,128]{1,0:T(8,128)(2,1)S(1)}, bf16[512,128]{1,0:T(8,128)(2,1)S(1)}, u32[]{:S(2)}, u32[]{:S(2)}) collective-permute-start(bf16[512,128]{1,0:T(8,128)(2,1)S(1)} %collective-permute-done.21.refs_2_), channel_id=1, source_target_pairs={{0,1},{1,0},{2,3},{3,2},{4,5},{5,4},{6,7},{7,6},{8,9},{9,8},{10,11... | collective-permute-start | bytes 393224 | tf_op jit(solution)/shard_map/ppermute | solution.py:215
  124.3 1.8 collective-permute-start.27
  127.5 2.5 %all_gather.29.pair = bf16[1024,128]{1,0:T(8,128)(2,1)S(1)} all-gather(bf16[512,128]{1,0:T(8,128)(2,1)S(1)} %get-tuple-element.87.piece), channel_id=1, replica_groups={{0,1},{2,3},{4,5},{6,7},{8,9},{10,11},{12,13},{14,15},{16,17},{18,19},{..., dimensions={0}, use_global_device_ids=true | all-gather | bytes 393216 | tf_op jit(solution)/shard_map/all_gather | solution.py:197
  136.4 20.7 %all_to_all.22.mine = bf16[32,64,128]{2,1,0:T(8,128)(2,1)S(1)} all-to-all(bf16[32,64,128]{2,1,0:T(8,128)(2,1)S(1)} %get-tuple-element.92), channel_id=1, replica_groups=mesh['area'=32,'unit'=8] {'area'}, dimensions={0} | all-to-all | bytes 1048576 | tf_op jit(solution)/shard_map/all_to_all | solution.py:253
  157.1 2.1 collective-permute-start.31
  159.2 1.9 shard_map.137.partial
  166.0 2.5 %all_gather.30.pair = bf16[1024,128]{1,0:T(8,128)(2,1)S(1)} all-gather(bf16[512,128]{1,0:T(8,128)(2,1)S(1)} %get-tuple-element.96.piece), channel_id=1, replica_groups={{0,1},{2,3},{4,5},{6,7},{8,9},{10,11},{12,13},{14,15},{16,17},{18,19},{..., dimensions={0}, use_global_device_ids=true | all-gather | bytes 393216 | tf_op jit(solution)/shard_map/all_gather | solution.py:197
  169.1 2.2 %collective-permute-start.35 = (bf16[512,128]{1,0:T(8,128)(2,1)S(1)}, bf16[512,128]{1,0:T(8,128)(2,1)S(1)}, u32[]{:S(2)}, u32[]{:S(2)}) collective-permute-start(bf16[512,128]{1,0:T(8,128)(2,1)S(1)} %collective-permute-done.34.refs_2_), channel_id=1, source_target_pairs={{0,1},{1,0},{2,3},{3,2},{4,5},{5,4},{6,7},{7,6},{8,9},{9,8},{10,11... | collective-permute-start | bytes 393224 | tf_op jit(solution)/shard_map/ppermute | solution.py:215
  174.5 2.2 %shard_map.140 = (bf16[4096,128]{1,0:T(8,128)(2,1)S(1)}, f32[512,128]{1,0:T(8,128)}, bf16[512,128]{1,0:T(8,128)(2,1)S(1)}) custom-call(s32[64]{0:T(128)S(1)} %pad_add_fusion.table, bf16[512,4096]{1,0:T(8,128)(2,1)S(1)} %bitcast.32, bf16[512,128]{1,0:T(8,128)(2,1)S(1)} %collective-permute-done.32.refs_0_, ...), custom_call_target="tpu_custom_call" | custom-call | flops 268435456 | bytes 5769472 | tf_op jit(solution)/shard_map/pallas_call | solution.py:180
  176.7 1.8 collective-permute-start.40
  180.0 2.5 %all_gather.31.pair = bf16[1024,128]{1,0:T(8,128)(2,1)S(1)} all-gather(bf16[512,128]{1,0:T(8,128)(2,1)S(1)} %get-tuple-element.104.piece), channel_id=1, replica_groups={{0,1},{2,3},{4,5},{6,7},{8,9},{10,11},{12,13},{14,15},{16,17},{18,19},{..., dimensions={0}, use_global_device_ids=true | all-gather | bytes 393216 | tf_op jit(solution)/shard_map/all_gather | solution.py:197
  183.1 1.9 collective-permute-start.41
  186.8 1.9 shard_map.141
  190.4 20.8 %all_to_all.23.mine = bf16[32,64,128]{2,1,0:T(8,128)(2,1)S(1)} all-to-all(bf16[32,64,128]{2,1,0:T(8,128)(2,1)S(1)} %get-tuple-element.109), channel_id=1, replica_groups=mesh['area'=32,'unit'=8] {'area'}, dimensions={0} | all-to-all | bytes 1048576 | tf_op jit(solution)/shard_map/all_to_all | solution.py:253
  211.2 2.0 collective-permute-start.44
  214.8 2.2 %shard_map.143 = f32[512,128]{1,0:T(8,128)} custom-call(s32[64]{0:T(128)S(1)} %pad_add_fusion.table, bf16[512,2048]{1,0:T(8,128)(2,1)S(1)} %bitcast.36, bf16[32,64,128]{2,1,0:T(8,128)(2,1)S(1)} %all_to_all.23.mine, bf16[32,64,128]{2,1,0:T(8,128)(2,1)S(1)} %collective-permute-done.44.theirs), custom_call_target="tpu_custom_call" | custom-call | flops 268435456 | bytes 3145984 | tf_op jit(solution)/shard_map/pallas_call | solution.py:180
  (118 shorter events, 62.3 us)
Async XLA Ops:
  2.5 15.3 %collective-permute-start.4 = (bf16[1024,128]{1,0:T(8,128)(2,1)S(1)}, bf16[1024,128]{1,0:T(8,128)(2,1)S(1)}, u32[]{:S(2)}, u32[]{:S(2)}) collective-permute-start(bf16[1024,128]{1,0:T(8,128)(2,1)S(1)} %shard_map.122.own), channel_id=1, source_target_pairs={{0,6},{1,7},{2,4},{3,5},{4,2},{5,3},{6,0},{7,1},{8,14},{9,15},{10,... | collective-permute-start | bytes 786440 | tf_op jit(solution)/shard_map/ppermute | solution.py:206
  6.2 11.6 %collective-permute-start.2 = (bf16[1024,128]{1,0:T(8,128)(2,1)S(1)}, bf16[1024,128]{1,0:T(8,128)(2,1)S(1)}, u32[]{:S(2)}, u32[]{:S(2)}) collective-permute-start(bf16[1024,128]{1,0:T(8,128)(2,1)S(1)} %shard_map.122.own), channel_id=1, source_target_pairs={{0,4},{1,5},{2,6},{3,7},{4,0},{5,1},{6,2},{7,3},{8,12},{9,13},{10,... | collective-permute-start | bytes 786440 | tf_op jit(solution)/shard_map/ppermute | solution.py:206
  6.5 14.3 %collective-permute-start.1 = (bf16[1024,128]{1,0:T(8,128)(2,1)S(1)}, bf16[1024,128]{1,0:T(8,128)(2,1)}, u32[]{:S(2)}, u32[]{:S(2)}) collective-permute-start(bf16[1024,128]{1,0:T(8,128)(2,1)S(1)} %shard_map.122.own), channel_id=1, source_target_pairs={{0,2},{1,3},{2,0},{3,1},{4,6},{5,7},{6,4},{7,5},{8,10},{9,11},{10,... | collective-permute-start | bytes 786440 | tf_op jit(solution)/shard_map/ppermute | solution.py:206
  6.8 16.4 %collective-permute-start = (bf16[1024,128]{1,0:T(8,128)(2,1)S(1)}, bf16[1024,128]{1,0:T(8,128)(2,1)S(1)}, u32[]{:S(2)}, u32[]{:S(2)}) collective-permute-start(bf16[1024,128]{1,0:T(8,128)(2,1)S(1)} %shard_map.122.own), channel_id=1, source_target_pairs={{0,1},{1,0},{2,3},{3,2},{4,5},{5,4},{6,7},{7,6},{8,9},{9,8},{10,11... | collective-permute-start | bytes 786440 | tf_op jit(solution)/shard_map/ppermute | solution.py:263
  17.8 5.4 %collective-permute-start.3 = (bf16[1024,128]{1,0:T(8,128)(2,1)S(1)}, bf16[1024,128]{1,0:T(8,128)(2,1)S(1)}, u32[]{:S(2)}, u32[]{:S(2)}) collective-permute-start(bf16[1024,128]{1,0:T(8,128)(2,1)S(1)} %collective-permute-done.2.far), channel_id=1, source_target_pairs={{0,1},{1,0},{2,3},{3,2},{4,5},{5,4},{6,7},{7,6},{8,9},{9,8},{10,11... | collective-permute-start | bytes 786440 | tf_op jit(solution)/shard_map/ppermute | solution.py:265
  58.1 6.1 %collective-permute-start.10 = (bf16[512,128]{1,0:T(8,128)(2,1)S(1)}, bf16[512,128]{1,0:T(8,128)(2,1)S(1)}, u32[]{:S(2)}, u32[]{:S(2)}) collective-permute-start(bf16[512,128]{1,0:T(8,128)(2,1)S(1)} %get-tuple-element.64.piece), channel_id=1, source_target_pairs={{0,2},{1,3},{2,0},{3,1},{4,6},{5,7},{6,4},{7,5},{8,10},{9,11},{10,... | collective-permute-start | bytes 393224 | tf_op jit(solution)/shard_map/ppermute | solution.py:206
  58.2 8.3 %collective-permute-start.8 = (bf16[512,128]{1,0:T(8,128)(2,1)S(1)}, bf16[512,128]{1,0:T(8,128)(2,1)S(1)}, u32[]{:S(2)}, u32[]{:S(2)}) collective-permute-start(bf16[512,128]{1,0:T(8,128)(2,1)S(1)} %get-tuple-element.64.piece), channel_id=1, source_target_pairs={{0,6},{1,7},{2,4},{3,5},{4,2},{5,3},{6,0},{7,1},{8,14},{9,15},{10,... | collective-permute-start | bytes 393224 | tf_op jit(solution)/shard_map/ppermute | solution.py:206
  61.0 7.5 %collective-permute-start.6 = (bf16[512,128]{1,0:T(8,128)(2,1)S(1)}, bf16[512,128]{1,0:T(8,128)(2,1)S(1)}, u32[]{:S(2)}, u32[]{:S(2)}) collective-permute-start(bf16[512,128]{1,0:T(8,128)(2,1)S(1)} %get-tuple-element.64.piece), channel_id=1, source_target_pairs={{0,4},{1,5},{2,6},{3,7},{4,0},{5,1},{6,2},{7,3},{8,12},{9,13},{10,... | collective-permute-start | bytes 393224 | tf_op jit(solution)/shard_map/ppermute | solution.py:206
  64.3 5.1 %collective-permute-start.11 = (bf16[512,128]{1,0:T(8,128)(2,1)S(1)}, bf16[512,128]{1,0:T(8,128)(2,1)S(1)}, u32[]{:S(2)}, u32[]{:S(2)}) collective-permute-start(bf16[512,128]{1,0:T(8,128)(2,1)S(1)} %collective-permute-done.10.refs_0_), channel_id=1, source_target_pairs={{0,1},{1,0},{2,3},{3,2},{4,5},{5,4},{6,7},{7,6},{8,9},{9,8},{10,11... | collective-permute-start | bytes 393224 | tf_op jit(solution)/shard_map/ppermute | solution.py:215
  72.3 5.8 %collective-permute-start.16 = (bf16[512,128]{1,0:T(8,128)(2,1)S(1)}, bf16[512,128]{1,0:T(8,128)(2,1)S(1)}, u32[]{:S(2)}, u32[]{:S(2)}) collective-permute-start(bf16[512,128]{1,0:T(8,128)(2,1)S(1)} %get-tuple-element.71.piece), channel_id=1, source_target_pairs={{0,2},{1,3},{2,0},{3,1},{4,6},{5,7},{6,4},{7,5},{8,10},{9,11},{10,... | collective-permute-start | bytes 393224 | tf_op jit(solution)/shard_map/ppermute | solution.py:206
  72.4 6.7 %collective-permute-start.14 = (bf16[512,128]{1,0:T(8,128)(2,1)S(1)}, bf16[512,128]{1,0:T(8,128)(2,1)S(1)}, u32[]{:S(2)}, u32[]{:S(2)}) collective-permute-start(bf16[512,128]{1,0:T(8,128)(2,1)S(1)} %get-tuple-element.71.piece), channel_id=1, source_target_pairs={{0,6},{1,7},{2,4},{3,5},{4,2},{5,3},{6,0},{7,1},{8,14},{9,15},{10,... | collective-permute-start | bytes 393224 | tf_op jit(solution)/shard_map/ppermute | solution.py:206
  74.1 7.0 %collective-permute-start.12 = (bf16[512,128]{1,0:T(8,128)(2,1)S(1)}, bf16[512,128]{1,0:T(8,128)(2,1)S(1)}, u32[]{:S(2)}, u32[]{:S(2)}) collective-permute-start(bf16[512,128]{1,0:T(8,128)(2,1)S(1)} %get-tuple-element.71.piece), channel_id=1, source_target_pairs={{0,4},{1,5},{2,6},{3,7},{4,0},{5,1},{6,2},{7,3},{8,12},{9,13},{10,... | collective-permute-start | bytes 393224 | tf_op jit(solution)/shard_map/ppermute | solution.py:206
  79.0 4.5 %collective-permute-start.15 = (bf16[512,128]{1,0:T(8,128)(2,1)S(1)}, bf16[512,128]{1,0:T(8,128)(2,1)S(1)}, u32[]{:S(2)}, u32[]{:S(2)}) collective-permute-start(bf16[512,128]{1,0:T(8,128)(2,1)S(1)} %collective-permute-done.14.refs_2_), channel_id=1, source_target_pairs={{0,1},{1,0},{2,3},{3,2},{4,5},{5,4},{6,7},{7,6},{8,9},{9,8},{10,11... | collective-permute-start | bytes 393224 | tf_op jit(solution)/shard_map/ppermute | solution.py:215
  110.8 5.8 %collective-permute-start.23 = (bf16[512,128]{1,0:T(8,128)(2,1)S(1)}, bf16[512,128]{1,0:T(8,128)(2,1)S(1)}, u32[]{:S(2)}, u32[]{:S(2)}) collective-permute-start(bf16[512,128]{1,0:T(8,128)(2,1)S(1)} %get-tuple-element.80.piece), channel_id=1, source_target_pairs={{0,2},{1,3},{2,0},{3,1},{4,6},{5,7},{6,4},{7,5},{8,10},{9,11},{10,... | collective-permute-start | bytes 393224 | tf_op jit(solution)/shard_map/ppermute | solution.py:206
  111.3 6.0 %collective-permute-start.21 = (bf16[512,128]{1,0:T(8,128)(2,1)S(1)}, bf16[512,128]{1,0:T(8,128)(2,1)S(1)}, u32[]{:S(2)}, u32[]{:S(2)}) collective-permute-start(bf16[512,128]{1,0:T(8,128)(2,1)S(1)} %get-tuple-element.80.piece), channel_id=1, source_target_pairs={{0,6},{1,7},{2,4},{3,5},{4,2},{5,3},{6,0},{7,1},{8,14},{9,15},{10,... | collective-permute-start | bytes 393224 | tf_op jit(solution)/shard_map/ppermute | solution.py:206
  112.9 7.5 %collective-permute-start.19 = (bf16[512,128]{1,0:T(8,128)(2,1)S(1)}, bf16[512,128]{1,0:T(8,128)(2,1)S(1)}, u32[]{:S(2)}, u32[]{:S(2)}) collective-permute-start(bf16[512,128]{1,0:T(8,128)(2,1)S(1)} %get-tuple-element.80.piece), channel_id=1, source_target_pairs={{0,4},{1,5},{2,6},{3,7},{4,0},{5,1},{6,2},{7,3},{8,12},{9,13},{10,... | collective-permute-start | bytes 393224 | tf_op jit(solution)/shard_map/ppermute | solution.py:206
  116.6 4.7 %collective-permute-start.24 = (bf16[512,128]{1,0:T(8,128)(2,1)S(1)}, bf16[512,128]{1,0:T(8,128)(2,1)S(1)}, u32[]{:S(2)}, u32[]{:S(2)}) collective-permute-start(bf16[512,128]{1,0:T(8,128)(2,1)S(1)} %collective-permute-done.23.refs_0_), channel_id=1, source_target_pairs={{0,1},{1,0},{2,3},{3,2},{4,5},{5,4},{6,7},{7,6},{8,9},{9,8},{10,11... | collective-permute-start | bytes 393224 | tf_op jit(solution)/shard_map/ppermute | solution.py:215
  117.3 5.4 %collective-permute-start.22 = (bf16[512,128]{1,0:T(8,128)(2,1)S(1)}, bf16[512,128]{1,0:T(8,128)(2,1)S(1)}, u32[]{:S(2)}, u32[]{:S(2)}) collective-permute-start(bf16[512,128]{1,0:T(8,128)(2,1)S(1)} %collective-permute-done.21.refs_2_), channel_id=1, source_target_pairs={{0,1},{1,0},{2,3},{3,2},{4,5},{5,4},{6,7},{7,6},{8,9},{9,8},{10,11... | collective-permute-start | bytes 393224 | tf_op jit(solution)/shard_map/ppermute | solution.py:215
  124.2 5.8 %collective-permute-start.29 = (bf16[512,128]{1,0:T(8,128)(2,1)S(1)}, bf16[512,128]{1,0:T(8,128)(2,1)S(1)}, u32[]{:S(2)}, u32[]{:S(2)}) collective-permute-start(bf16[512,128]{1,0:T(8,128)(2,1)S(1)} %get-tuple-element.87.piece), channel_id=1, source_target_pairs={{0,2},{1,3},{2,0},{3,1},{4,6},{5,7},{6,4},{7,5},{8,10},{9,11},{10,... | collective-permute-start | bytes 393224 | tf_op jit(solution)/shard_map/ppermute | solution.py:206
  124.3 6.7 %collective-permute-start.27 = (bf16[512,128]{1,0:T(8,128)(2,1)S(1)}, bf16[512,128]{1,0:T(8,128)(2,1)S(1)}, u32[]{:S(2)}, u32[]{:S(2)}) collective-permute-start(bf16[512,128]{1,0:T(8,128)(2,1)S(1)} %get-tuple-element.87.piece), channel_id=1, source_target_pairs={{0,6},{1,7},{2,4},{3,5},{4,2},{5,3},{6,0},{7,1},{8,14},{9,15},{10,... | collective-permute-start | bytes 393224 | tf_op jit(solution)/shard_map/ppermute | solution.py:206
  126.0 7.0 %collective-permute-start.25 = (bf16[512,128]{1,0:T(8,128)(2,1)S(1)}, bf16[512,128]{1,0:T(8,128)(2,1)S(1)}, u32[]{:S(2)}, u32[]{:S(2)}) collective-permute-start(bf16[512,128]{1,0:T(8,128)(2,1)S(1)} %get-tuple-element.87.piece), channel_id=1, source_target_pairs={{0,4},{1,5},{2,6},{3,7},{4,0},{5,1},{6,2},{7,3},{8,12},{9,13},{10,... | collective-permute-start | bytes 393224 | tf_op jit(solution)/shard_map/ppermute | solution.py:206
  130.0 4.3 %collective-permute-start.30 = (bf16[512,128]{1,0:T(8,128)(2,1)S(1)}, bf16[512,128]{1,0:T(8,128)(2,1)S(1)}, u32[]{:S(2)}, u32[]{:S(2)}) collective-permute-start(bf16[512,128]{1,0:T(8,128)(2,1)S(1)} %collective-permute-done.29.near), channel_id=1, source_target_pairs={{0,1},{1,0},{2,3},{3,2},{4,5},{5,4},{6,7},{7,6},{8,9},{9,8},{10,11... | collective-permute-start | bytes 393224 | tf_op jit(solution)/shard_map/ppermute | solution.py:215
  130.9 4.5 %collective-permute-start.28 = (bf16[512,128]{1,0:T(8,128)(2,1)S(1)}, bf16[512,128]{1,0:T(8,128)(2,1)S(1)}, u32[]{:S(2)}, u32[]{:S(2)}) collective-permute-start(bf16[512,128]{1,0:T(8,128)(2,1)S(1)} %collective-permute-done.27.refs_2_), channel_id=1, source_target_pairs={{0,1},{1,0},{2,3},{3,2},{4,5},{5,4},{6,7},{7,6},{8,9},{9,8},{10,11... | collective-permute-start | bytes 393224 | tf_op jit(solution)/shard_map/ppermute | solution.py:215
  162.6 5.8 %collective-permute-start.36 = (bf16[512,128]{1,0:T(8,128)(2,1)S(1)}, bf16[512,128]{1,0:T(8,128)(2,1)S(1)}, u32[]{:S(2)}, u32[]{:S(2)}) collective-permute-start(bf16[512,128]{1,0:T(8,128)(2,1)S(1)} %get-tuple-element.96.piece), channel_id=1, source_target_pairs={{0,2},{1,3},{2,0},{3,1},{4,6},{5,7},{6,4},{7,5},{8,10},{9,11},{10,... | collective-permute-start | bytes 393224 | tf_op jit(solution)/shard_map/ppermute | solution.py:206
  163.1 6.0 %collective-permute-start.34 = (bf16[512,128]{1,0:T(8,128)(2,1)S(1)}, bf16[512,128]{1,0:T(8,128)(2,1)S(1)}, u32[]{:S(2)}, u32[]{:S(2)}) collective-permute-start(bf16[512,128]{1,0:T(8,128)(2,1)S(1)} %get-tuple-element.96.piece), channel_id=1, source_target_pairs={{0,6},{1,7},{2,4},{3,5},{4,2},{5,3},{6,0},{7,1},{8,14},{9,15},{10,... | collective-permute-start | bytes 393224 | tf_op jit(solution)/shard_map/ppermute | solution.py:206
  164.7 7.5 %collective-permute-start.32 = (bf16[512,128]{1,0:T(8,128)(2,1)S(1)}, bf16[512,128]{1,0:T(8,128)(2,1)S(1)}, u32[]{:S(2)}, u32[]{:S(2)}) collective-permute-start(bf16[512,128]{1,0:T(8,128)(2,1)S(1)} %get-tuple-element.96.piece), channel_id=1, source_target_pairs={{0,4},{1,5},{2,6},{3,7},{4,0},{5,1},{6,2},{7,3},{8,12},{9,13},{10,... | collective-permute-start | bytes 393224 | tf_op jit(solution)/shard_map/ppermute | solution.py:206
  168.4 4.7 %collective-permute-start.37 = (bf16[512,128]{1,0:T(8,128)(2,1)S(1)}, bf16[512,128]{1,0:T(8,128)(2,1)S(1)}, u32[]{:S(2)}, u32[]{:S(2)}) collective-permute-start(bf16[512,128]{1,0:T(8,128)(2,1)S(1)} %collective-permute-done.36.refs_0_), channel_id=1, source_target_pairs={{0,1},{1,0},{2,3},{3,2},{4,5},{5,4},{6,7},{7,6},{8,9},{9,8},{10,11... | collective-permute-start | bytes 393224 | tf_op jit(solution)/shard_map/ppermute | solution.py:215
  169.1 5.4 %collective-permute-start.35 = (bf16[512,128]{1,0:T(8,128)(2,1)S(1)}, bf16[512,128]{1,0:T(8,128)(2,1)S(1)}, u32[]{:S(2)}, u32[]{:S(2)}) collective-permute-start(bf16[512,128]{1,0:T(8,128)(2,1)S(1)} %collective-permute-done.34.refs_2_), channel_id=1, source_target_pairs={{0,1},{1,0},{2,3},{3,2},{4,5},{5,4},{6,7},{7,6},{8,9},{9,8},{10,11... | collective-permute-start | bytes 393224 | tf_op jit(solution)/shard_map/ppermute | solution.py:215
  176.7 5.7 %collective-permute-start.42 = (bf16[512,128]{1,0:T(8,128)(2,1)S(1)}, bf16[512,128]{1,0:T(8,128)(2,1)S(1)}, u32[]{:S(2)}, u32[]{:S(2)}) collective-permute-start(bf16[512,128]{1,0:T(8,128)(2,1)S(1)} %get-tuple-element.104.piece), channel_id=1, source_target_pairs={{0,2},{1,3},{2,0},{3,1},{4,6},{5,7},{6,4},{7,5},{8,10},{9,11},{10,... | collective-permute-start | bytes 393224 | tf_op jit(solution)/shard_map/ppermute | solution.py:206
  176.7 6.4 %collective-permute-start.40 = (bf16[512,128]{1,0:T(8,128)(2,1)S(1)}, bf16[512,128]{1,0:T(8,128)(2,1)S(1)}, u32[]{:S(2)}, u32[]{:S(2)}) collective-permute-start(bf16[512,128]{1,0:T(8,128)(2,1)S(1)} %get-tuple-element.104.piece), channel_id=1, source_target_pairs={{0,6},{1,7},{2,4},{3,5},{4,2},{5,3},{6,0},{7,1},{8,14},{9,15},{10,... | collective-permute-start | bytes 393224 | tf_op jit(solution)/shard_map/ppermute | solution.py:206
  178.5 7.0 %collective-permute-start.38 = (bf16[512,128]{1,0:T(8,128)(2,1)S(1)}, bf16[512,128]{1,0:T(8,128)(2,1)S(1)}, u32[]{:S(2)}, u32[]{:S(2)}) collective-permute-start(bf16[512,128]{1,0:T(8,128)(2,1)S(1)} %get-tuple-element.104.piece), channel_id=1, source_target_pairs={{0,4},{1,5},{2,6},{3,7},{4,0},{5,1},{6,2},{7,3},{8,12},{9,13},{10,... | collective-permute-start | bytes 393224 | tf_op jit(solution)/shard_map/ppermute | solution.py:206
  183.1 5.6 %collective-permute-start.41 = (bf16[512,128]{1,0:T(8,128)(2,1)S(1)}, bf16[512,128]{1,0:T(8,128)(2,1)S(1)}, u32[]{:S(2)}, u32[]{:S(2)}) collective-permute-start(bf16[512,128]{1,0:T(8,128)(2,1)S(1)} %collective-permute-done.40.refs_2_), channel_id=1, source_target_pairs={{0,1},{1,0},{2,3},{3,2},{4,5},{5,4},{6,7},{7,6},{8,9},{9,8},{10,11... | collective-permute-start | bytes 393224 | tf_op jit(solution)/shard_map/ppermute | solution.py:215
  (22 other events, 84.7 us)
where the time goes:
time: 217 us
  blocking collectives  110 us (51%)
  starting transfers between devices  56.9 us (26%)
  Pallas kernels  32.5 us (15%)
  waiting for transfers between devices  8.38 us (4%)
  local copies, waits for them, and re-layouts  7.45 us (3%)
    all_to_all x4, blocking collectives, long_range(): lax.all_to_all(outgoing, 'area', split_axis=0, concat_axis=0, tiled=True)  90 us
    pallas_call x22, Pallas kernels, call(): pl.pallas_call(kernel, out_shape=outs, in_specs=[SMEM if x.dtype == jnp.i...  32.5 us
    ppermute x21, starting transfers between devices, neighbours(): found.append(lax.ppermute(piece, 'unit', [(u, u ^ m) for u in range(8)]))  24.9 us
    ppermute x18, starting transfers between devices, exchange(): pieces += [x, lax.ppermute(x, 'unit', PAIRS)]  20.6 us
    all_gather x8, blocking collectives, paired(): lax.all_gather(piece, 'unit', axis=0, tiled=True, axis_index_groups=[[0,...  19.9 us
    ppermute x4, starting transfers between devices, long_range(): other = lax.ppermute(arrived, 'unit', [(u, u ^ 1) for u in range(8)])  8.36 us
    ppermute x21, waiting for transfers between devices, neighbours(): found.append(lax.ppermute(piece, 'unit', [(u, u ^ m) for u in range(8)]))  6.78 us
    unnamed x18, local copies, waits for them, and re-layouts  5.51 us
  transfers between devices with their start and end apart: 45, of which 10 were waited for; matrix products, arithmetic and copies ran while one was open for 1% of the time, Pallas kernels for 7%

commit v1 on v0

--- a/solution.py
+++ b/solution.py
@@ -41,10 +41,11 @@
     lax.fori_loop(0, 2, one, 0)
 
 
-def send(table, sources, outgoing):
+def send(table, lists, counts, stage, sources, outgoing):
     half = table[CORE] * HALF
 
-    def one(area, carry):
+    def one(i, carry):
+        area = lists[stage, i]
         row = table[area]
         for array, first in sources:
             count = array.shape[0] // BLOCK
@@ -56,41 +57,56 @@
 
         return carry
 
-    lax.fori_loop(0, BLOCKS, one, 0, unroll=4)
+    lax.fori_loop(0, counts[stage], one, 0)
 
 
 def product(table, weight, rows, full, first):
     total = None
     for m in range(full.shape[0] // ROWS):
-        columns = pl.ds(pl.multiple_of(table[UNIT + first + m], ROWS), ROWS)
+        columns = pl.ds(pl.multiple_of(table[UNIT + first + m] * ROWS, ROWS), ROWS)
         part = jnp.dot(weight[rows, columns], full[m * ROWS : (m + 1) * ROWS, :], preferred_element_type=F32)
         total = part if total is None else total + part
     return total
 
 
-def begin_kernel(table, piece, pair, near, near_other, earlier, front, outgoing):
+def begin_kernel(table, lists, counts, piece, pair, near, near_other, earlier, front, outgoing):
     put_own(table, piece, pair, front)
     put((near, near_other), 2, front)
-    send(table, ((front, 0), (earlier, BLOCKS)), outgoing)
-
-
-def finish_kernel(table, *refs):
+    send(table, lists, counts, 0, ((front, 0), (earlier, BLOCKS)), outgoing)
+
+
+def finish_kernel(table, lists, counts, *refs):
     *pieces, begun, back, outgoing = refs
     del begun
     put(pieces, 0, back)
-    send(table, ((back, BLOCKS // 2),), outgoing)
-
-
-def start_kernel(table, own, other, near, far, far_other, second, front, back, outgoing, earlier):
+    send(table, lists, counts, 1, ((back, BLOCKS // 2),), outgoing)
+
+
+def last_begin_kernel(*refs):
+    *inputs, outgoing, front = refs
+    begin_kernel(*inputs, front, outgoing)
+
+
+def last_finish_kernel(*refs):
+    *inputs, outgoing, back = refs
+    finish_kernel(*inputs, back, outgoing)
+
+
+def copy_kernel(source, out):
+    out[...] = source[...]
+
+
+def start_kernel(table, lists, counts, own, near, far, far_other, second, front, back, outgoing, earlier):
     mine = pl.multiple_of(table[CORE] * 2 * ROWS, 2 * ROWS)
     theirs = pl.multiple_of(2 * ROWS - mine, 2 * ROWS)
     for m, (piece, row) in enumerate(
-        ((own, 0), (other, 0), (near, mine), (near, theirs), (far, 0), (far_other, 0), (second, mine), (second, theirs))
+        ((own, mine), (own, theirs), (near, mine), (near, theirs), (far, 0), (far_other, 0), (second, mine), (second, theirs))
     ):
         full, first = (front, m * ROWS) if m < 4 else (back, (m - 4) * ROWS)
         full[first : first + ROWS, :] = piece[pl.ds(row, ROWS), :]
         earlier[m * ROWS : (m + 1) * ROWS, :] = piece[pl.ds(row + ROWS, ROWS), :]
-    send(table, ((front, 0), (back, BLOCKS // 2), (earlier, BLOCKS)), outgoing)
+    send(table, lists, counts, 0, ((front, 0), (earlier, BLOCKS)), outgoing)
+    send(table, lists, counts, 1, ((back, BLOCKS // 2),), outgoing)
 
 
 def local_kernel(table, weight, front, back, drive, out):
@@ -158,13 +174,18 @@
         copy[rows, :] = new.astype(BF16)
 
 
+def column(row):
+    return jnp.transpose(jnp.broadcast_to(row, (BLOCK, row.shape[1])))
+
+
 def drive_kernel(weight, stimulus, bias, leak, local_weight, out, leak_out):
     del local_weight
-    leak_out[...] = leak[...]
+    leak_out[...] = column(leak[...])
+    base = column(bias[...])
 
     def one(n, carry):
         part = lax.dot_general(weight[...], stimulus[n], (((0,), (0,)), ((), ())), preferred_element_type=F32)
-        out[n] = part + bias[...]
+        out[n] = part + base
         return carry
 
     lax.fori_loop(0, 2 * WINDOWS, one, 0)
@@ -238,20 +259,31 @@
     send_rows = jnp.sum(jnp.where(from_here, block_row, 0), axis=1)
     own_source = lax.dynamic_index_in_dim(link_source, area_here, 0, keepdims=False)
     core = jnp.full((8,), unit_here % 2, jnp.int32)
-    table = jnp.concatenate([send_rows, own_source, core, order * ROWS]).astype(jnp.int32)
+    live = jnp.any(from_here, axis=1)
+    late = (send_rows >= BLOCKS // 2) & (send_rows < BLOCKS)
+    areas = jnp.arange(BLOCKS, dtype=jnp.int32)
+    stages = jnp.arange(2, dtype=jnp.int32)
+    chosen = live[None, :] & (late.astype(jnp.int32)[None, :] == stages[:, None])
+    ahead = chosen[:, None, :] & (areas[None, None, :] < areas[None, :, None])
+    place = jnp.sum(ahead.astype(jnp.int32), axis=2)
+    here = chosen[:, None, :] & (place[:, None, :] == areas[None, :, None])
+    lists = jnp.sum(jnp.where(here, areas[None, None, :], 0), axis=2).astype(jnp.int32)
+    counts = jnp.sum(chosen.astype(jnp.int32), axis=1).astype(jnp.int32)
+    table = jnp.concatenate([send_rows, own_source, core, order]).astype(jnp.int32)
+    tables = [table, lists, counts]
     weight_local = local_weight[0]
     weight_long = long_weight[0]
     drives, leak = call(
         drive_kernel,
-        [input_weight[0].T, stimulus, unit_bias[0][:, None], leak_rate[0][:, None], weight_local],
-        (jax.ShapeDtypeStruct((2 * WINDOWS, ROWS, BLOCK), F32), jax.ShapeDtypeStruct((ROWS, 1), F32)),
+        [input_weight[0].T, stimulus, unit_bias, leak_rate, weight_local],
+        (jax.ShapeDtypeStruct((2 * WINDOWS, ROWS, BLOCK), F32), shape(ROWS, F32)),
         1000,
     )
     flops = ROWS * UNITS * BLOCK
 
     def long_range(outgoing):
         arrived = lax.all_to_all(outgoing, "area", split_axis=0, concat_axis=0, tiled=True)
-        other = lax.ppermute(arrived, "unit", [(u, u ^ 1) for u in range(8)])
+        other = lax.ppermute(arrived, "unit", PAIRS)
         return arrived, other
 
     gather_scratch = [pltpu.VMEM((16 * BLOCK, BLOCK), BF16)]
@@ -260,11 +292,12 @@
     half_history = shape(UNITS // 2, BF16)
     both = call(both_kernel, [initial_rates[0], prior_rates[0]], shape(2 * ROWS, BF16), 1000)
     near, second, far = neighbours(both)
-    other = lax.ppermute(both, "unit", PAIRS)
+    own = paired(both)
     far, drives, leak = lax.optimization_barrier((far, drives, leak))
-    pairs = [both, other, paired(near), far, lax.ppermute(far, "unit", PAIRS), paired(second)]
+    near = paired(near)
+    pairs = [own, near, far, lax.ppermute(far, "unit", PAIRS), paired(second)]
     *later, outgoing = call(
-        start_kernel, [table, *pairs], (half_history, half_history, parcels), 1000, [pltpu.VMEM((UNITS, BLOCK), BF16)]
+        start_kernel, [*tables, *pairs], (half_history, half_history, parcels), 1000, [pltpu.VMEM((UNITS, BLOCK), BF16)]
     )
 
     def window(step, carry):
@@ -293,10 +326,14 @@
             flops,
         )
         pieces = exchange(copy)
-        front, outgoing = call(begin_kernel, [table, *pieces[:4], earlier], (half_history, parcels), 1000)
-        back, outgoing = call(
-            finish_kernel, [table, *pieces[4:], outgoing], (half_history, parcels), 1000, aliases={5: 1}
-        )
+        if step == WINDOWS - 1:
+            scratch = [pltpu.VMEM((UNITS // 2, BLOCK), BF16)]
+            outgoing = call(last_begin_kernel, [*tables, *pieces[:4], earlier], parcels, 1000, scratch)
+            inputs = [*tables, *pieces[4:], outgoing]
+            return None, call(last_finish_kernel, inputs, parcels, 1000, scratch, {7: 0}), rates
+        keep = ((half_history, parcels), 1000)
+        front, outgoing = call(begin_kernel, [*tables, *pieces[:4], earlier], *keep)
+        back, outgoing = call(finish_kernel, [*tables, *pieces[4:], outgoing], *keep, aliases={7: 1})
         later = [front, back]
         return later, outgoing, rates
 
@@ -305,6 +342,7 @@
         carry = window(step, carry)
     later, outgoing, rates = carry
     mine, theirs = long_range(outgoing)
+    rates = call(copy_kernel, [rates], shape(ROWS, F32), 1000)
     final_current = call(current_kernel, [table, weight_long, mine, theirs], shape(ROWS, F32), flops, gather_scratch)
     return (rates[None], final_current[None])
 

time: 217 us -> 216 us (level)
  blocking collectives: 110 us -> 114 us
  Pallas kernels: 32.5 us -> 28.6 us
  starting transfers between devices: 56.9 us -> 54.7 us
    all_gather x8 -> x9, blocking collectives: 19.9 us -> 23.7 us  [paired(): lax.all_gather(piece, 'unit', axis=0, tiled=True, axis_index_groups=[[0,...]
    pallas_call x22 -> x23, Pallas kernels: 32.5 us -> 28.6 us  [call(): pl.pallas_call(kernel, out_shape=outs, in_specs=[SMEM if x.dtype == jnp.i...]
    ppermute x6 -> x5, starting transfers between devices: 11.5 us -> 8.17 us  [the longest x4 7.8 us: long_range(): other = lax.ppermute(arrived, 'unit', PAIRS)]
    unnamed x18 -> x20, local copies, waits for them, and re-layouts: 5.51 us -> 6.87 us
  transfers between devices with their start and end apart: 45 -> 44, of which waited for: 10 -> 12; matrix products, arithmetic and copies ran while one was open for 1% -> 1% of each run, Pallas kernels for 7% -> 7%
where the time goes in v1:
time: 216 us; the launch traced here: 215 us
  blocking collectives  114 us (53%)
  starting transfers between devices  54.7 us (25%)
  Pallas kernels  28.6 us (13%)
  local copies, waits for them, and re-layouts  7.86 us (4%)
  waiting for transfers between devices  7.28 us (3%)
    all_to_all x4, blocking collectives, long_range(): lax.all_to_all(outgoing, 'area', split_axis=0, concat_axis=0, tiled=True)  90.3 us
    pallas_call x23, Pallas kernels, call(): pl.pallas_call(kernel, out_shape=outs, in_specs=[SMEM if x.dtype == jnp.i...  28.6 us
    ppermute x21, starting transfers between devices, neighbours(): found.append(lax.ppermute(piece, 'unit', [(u, u ^ m) for u in range(8)]))  25 us
    all_gather x9, blocking collectives, paired(): lax.all_gather(piece, 'unit', axis=0, tiled=True, axis_index_groups=[[0,...  23.7 us
    ppermute x18, starting transfers between devices, exchange(): pieces += [x, lax.ppermute(x, 'unit', PAIRS)]  21.5 us
    ppermute x4, starting transfers between devices, long_range(): other = lax.ppermute(arrived, 'unit', PAIRS)  7.8 us
    unnamed x20, local copies, waits for them, and re-layouts  6.87 us
    ppermute x21, waiting for transfers between devices, neighbours(): found.append(lax.ppermute(piece, 'unit', [(u, u ^ m) for u in range(8)]))  5.86 us
  transfers between devices with their start and end apart: 44, of which 12 were waited for; matrix products, arithmetic and copies ran while one was open for 1% of the time, Pallas kernels for 7%

profile of v1, /device:TPU:1, one launch (start us, length us, event | category | flops | bytes accessed | tf_op | source)
XLA Modules:
  0.0 215.4 jit_solution(12017870933356681871)
XLA Ops:
  2.5 3.6 %collective-permute-start.3 = (bf16[1024,128]{1,0:T(8,128)(2,1)S(1)}, bf16[1024,128]{1,0:T(8,128)(2,1)S(1)}, u32[]{:S(2)}, u32[]{:S(2)}) collective-permute-start(bf16[1024,128]{1,0:T(8,128)(2,1)S(1)} %shard_map.122), channel_id=1, source_target_pairs={{0,6},{1,7},{2,4},{3,5},{4,2},{5,3},{6,0},{7,1},{8,14},{9,15},{10,... | collective-permute-start | bytes 786440 | tf_op jit(solution)/shard_map/ppermute | solution.py:227
  9.5 2.2 %copy-done = bf16[1,512,4096]{2,1,0:T(8,128)(2,1)S(1)} copy-done((bf16[1,512,4096]{2,1,0:T(8,128)(2,1)S(1)}, bf16[1,512,4096]{2,1,0:T(8,128)(2,1)}, u32[]{:S(2)}) %copy-start) | copy-done | bytes 4194328
  16.2 4.9 %all_gather.27.own = bf16[2048,128]{1,0:T(8,128)(2,1)S(1)} all-gather(bf16[1024,128]{1,0:T(8,128)(2,1)S(1)} %shard_map.122), channel_id=1, replica_groups={{0,1},{2,3},{4,5},{6,7},{8,9},{10,11},{12,13},{14,15},{16,17},{18,19},{..., dimensions={0}, use_global_device_ids=true | all-gather | bytes 786432 | tf_op jit(solution)/shard_map/all_gather | solution.py:218
  21.5 2.2 %all_gather.29.second = bf16[2048,128]{1,0:T(8,128)(2,1)S(1)} all-gather(bf16[1024,128]{1,0:T(8,128)(2,1)S(1)} %collective-permute-done.3), channel_id=1, replica_groups={{0,1},{2,3},{4,5},{6,7},{8,9},{10,11},{12,13},{14,15},{16,17},{18,19},{..., dimensions={0}, use_global_device_ids=true | all-gather | bytes 786432 | tf_op jit(solution)/shard_map/all_gather | solution.py:218
  23.6 2.2 %all_gather.28.near = bf16[2048,128]{1,0:T(8,128)(2,1)S(1)} all-gather(bf16[1024,128]{1,0:T(8,128)(2,1)S(1)} %collective-permute-done), channel_id=1, replica_groups={{0,1},{2,3},{4,5},{6,7},{8,9},{10,11},{12,13},{14,15},{16,17},{18,19},{..., dimensions={0}, use_global_device_ids=true | all-gather | bytes 786432 | tf_op jit(solution)/shard_map/all_gather | solution.py:218
  26.7 26.6 %all_to_all.20.mine = bf16[32,64,128]{2,1,0:T(8,128)(2,1)S(1)} all-to-all(bf16[32,64,128]{2,1,0:T(8,128)(2,1)S(1)} %get-tuple-element.57), channel_id=1, replica_groups=mesh['area'=32,'unit'=8] {'area'}, dimensions={0} | all-to-all | bytes 1048576 | tf_op jit(solution)/shard_map/all_to_all | solution.py:285
  53.4 2.0 collective-permute-start.4
  55.5 2.0 shard_map.125.partial
  60.3 1.9 collective-permute-start.7
  63.0 2.2 %all_gather.30.pair = bf16[1024,128]{1,0:T(8,128)(2,1)S(1)} all-gather(bf16[512,128]{1,0:T(8,128)(2,1)S(1)} %get-tuple-element.62.piece), channel_id=1, replica_groups={{0,1},{2,3},{4,5},{6,7},{8,9},{10,11},{12,13},{14,15},{16,17},{18,19},{..., dimensions={0}, use_global_device_ids=true | all-gather | bytes 393216 | tf_op jit(solution)/shard_map/all_gather | solution.py:218
  65.5 2.0 collective-permute-done.7.refs_2_
  73.3 2.0 collective-permute-start.13
  76.6 2.5 %all_gather.31.pair = bf16[1024,128]{1,0:T(8,128)(2,1)S(1)} all-gather(bf16[512,128]{1,0:T(8,128)(2,1)S(1)} %get-tuple-element.69.piece), channel_id=1, replica_groups={{0,1},{2,3},{4,5},{6,7},{8,9},{10,11},{12,13},{14,15},{16,17},{18,19},{..., dimensions={0}, use_global_device_ids=true | all-gather | bytes 393216 | tf_op jit(solution)/shard_map/all_gather | solution.py:218
  79.8 2.1 collective-permute-start.14
  85.3 21.3 %all_to_all.21.mine = bf16[32,64,128]{2,1,0:T(8,128)(2,1)S(1)} all-to-all(bf16[32,64,128]{2,1,0:T(8,128)(2,1)S(1)} %get-tuple-element.74), channel_id=1, replica_groups=mesh['area'=32,'unit'=8] {'area'}, dimensions={0} | all-to-all | bytes 1048576 | tf_op jit(solution)/shard_map/all_to_all | solution.py:285
  106.5 1.9 collective-permute-start.17
  108.5 1.9 shard_map.131.partial
  112.1 1.9 collective-permute-start.20
  115.3 2.5 %all_gather.32.pair = bf16[1024,128]{1,0:T(8,128)(2,1)S(1)} all-gather(bf16[512,128]{1,0:T(8,128)(2,1)S(1)} %get-tuple-element.78.piece), channel_id=1, replica_groups={{0,1},{2,3},{4,5},{6,7},{8,9},{10,11},{12,13},{14,15},{16,17},{18,19},{..., dimensions={0}, use_global_device_ids=true | all-gather | bytes 393216 | tf_op jit(solution)/shard_map/all_gather | solution.py:218
  118.4 2.1 collective-permute-start.21
  128.5 2.5 %all_gather.33.pair = bf16[1024,128]{1,0:T(8,128)(2,1)S(1)} all-gather(bf16[512,128]{1,0:T(8,128)(2,1)S(1)} %get-tuple-element.85.piece), channel_id=1, replica_groups={{0,1},{2,3},{4,5},{6,7},{8,9},{10,11},{12,13},{14,15},{16,17},{18,19},{..., dimensions={0}, use_global_device_ids=true | all-gather | bytes 393216 | tf_op jit(solution)/shard_map/all_gather | solution.py:218
  131.6 1.9 collective-permute-start.27
  137.0 21.2 %all_to_all.22.mine = bf16[32,64,128]{2,1,0:T(8,128)(2,1)S(1)} all-to-all(bf16[32,64,128]{2,1,0:T(8,128)(2,1)S(1)} %get-tuple-element.90), channel_id=1, replica_groups=mesh['area'=32,'unit'=8] {'area'}, dimensions={0} | all-to-all | bytes 1048576 | tf_op jit(solution)/shard_map/all_to_all | solution.py:285
  158.2 1.9 collective-permute-start.30
  160.1 1.9 shard_map.137.partial
  166.9 2.5 %all_gather.34.pair = bf16[1024,128]{1,0:T(8,128)(2,1)S(1)} all-gather(bf16[512,128]{1,0:T(8,128)(2,1)S(1)} %get-tuple-element.94.piece), channel_id=1, replica_groups={{0,1},{2,3},{4,5},{6,7},{8,9},{10,11},{12,13},{14,15},{16,17},{18,19},{..., dimensions={0}, use_global_device_ids=true | all-gather | bytes 393216 | tf_op jit(solution)/shard_map/all_gather | solution.py:218
  170.0 2.1 collective-permute-start.34
  180.2 2.5 %all_gather.35.refs_4_ = bf16[1024,128]{1,0:T(8,128)(2,1)S(1)} all-gather(bf16[512,128]{1,0:T(8,128)(2,1)S(1)} %get-tuple-element.102.refs_3_), channel_id=1, replica_groups={{0,1},{2,3},{4,5},{6,7},{8,9},{10,11},{12,13},{14,15},{16,17},{18,19},{..., dimensions={0}, use_global_device_ids=true | all-gather | bytes 393216 | tf_op jit(solution)/shard_map/all_gather | solution.py:218
  183.3 1.9 collective-permute-start.40
  188.6 21.2 %all_to_all.23.mine = bf16[32,64,128]{2,1,0:T(8,128)(2,1)S(1)} all-to-all(bf16[32,64,128]{2,1,0:T(8,128)(2,1)S(1)} %shard_map.143), channel_id=1, replica_groups=mesh['area'=32,'unit'=8] {'area'}, dimensions={0} | all-to-all | bytes 1048576 | tf_op jit(solution)/shard_map/all_to_all | solution.py:285
  209.8 1.9 collective-permute-start.43
  213.3 2.2 %shard_map.144 = f32[512,128]{1,0:T(8,128)} custom-call(s32[64]{0:T(128)S(1)} %pad_add_fusion.table.refs_0_, bf16[512,2048]{1,0:T(8,128)(2,1)S(1)} %bitcast.34, bf16[32,64,128]{2,1,0:T(8,128)(2,1)S(1)} %all_to_all.23.mine, bf16[32,64,128]{2,1,0:T(8,128)(2,1)S(1)} %collective-permute-done.43.theirs), custom_call_target="tpu_custom_call" | custom-call | flops 268435456 | bytes 3145984 | tf_op jit(solution)/shard_map/pallas_call | solution.py:201
  (124 shorter events, 60.9 us)
Async XLA Ops:
  2.5 19.0 %collective-permute-start.3 = (bf16[1024,128]{1,0:T(8,128)(2,1)S(1)}, bf16[1024,128]{1,0:T(8,128)(2,1)S(1)}, u32[]{:S(2)}, u32[]{:S(2)}) collective-permute-start(bf16[1024,128]{1,0:T(8,128)(2,1)S(1)} %shard_map.122), channel_id=1, source_target_pairs={{0,6},{1,7},{2,4},{3,5},{4,2},{5,3},{6,0},{7,1},{8,14},{9,15},{10,... | collective-permute-start | bytes 786440 | tf_op jit(solution)/shard_map/ppermute | solution.py:227
  6.2 14.9 %collective-permute-start.1 = (bf16[1024,128]{1,0:T(8,128)(2,1)S(1)}, bf16[1024,128]{1,0:T(8,128)(2,1)S(1)}, u32[]{:S(2)}, u32[]{:S(2)}) collective-permute-start(bf16[1024,128]{1,0:T(8,128)(2,1)S(1)} %shard_map.122), channel_id=1, source_target_pairs={{0,4},{1,5},{2,6},{3,7},{4,0},{5,1},{6,2},{7,3},{8,12},{9,13},{10,... | collective-permute-start | bytes 786440 | tf_op jit(solution)/shard_map/ppermute | solution.py:227
  6.5 17.1 %collective-permute-start = (bf16[1024,128]{1,0:T(8,128)(2,1)S(1)}, bf16[1024,128]{1,0:T(8,128)(2,1)S(1)}, u32[]{:S(2)}, u32[]{:S(2)}) collective-permute-start(bf16[1024,128]{1,0:T(8,128)(2,1)S(1)} %shard_map.122), channel_id=1, source_target_pairs={{0,2},{1,3},{2,0},{3,1},{4,6},{5,7},{6,4},{7,5},{8,10},{9,11},{10,... | collective-permute-start | bytes 786440 | tf_op jit(solution)/shard_map/ppermute | solution.py:227
  21.1 4.7 %collective-permute-start.2 = (bf16[1024,128]{1,0:T(8,128)(2,1)S(1)}, bf16[1024,128]{1,0:T(8,128)(2,1)S(1)}, u32[]{:S(2)}, u32[]{:S(2)}) collective-permute-start(bf16[1024,128]{1,0:T(8,128)(2,1)S(1)} %collective-permute-done.1.far), channel_id=1, source_target_pairs={{0,1},{1,0},{2,3},{3,2},{4,5},{5,4},{6,7},{7,6},{8,9},{9,8},{10,11... | collective-permute-start | bytes 786440 | tf_op jit(solution)/shard_map/ppermute | solution.py:298
  59.0 6.2 %collective-permute-start.9 = (bf16[512,128]{1,0:T(8,128)(2,1)S(1)}, bf16[512,128]{1,0:T(8,128)(2,1)S(1)}, u32[]{:S(2)}, u32[]{:S(2)}) collective-permute-start(bf16[512,128]{1,0:T(8,128)(2,1)S(1)} %get-tuple-element.62.piece), channel_id=1, source_target_pairs={{0,2},{1,3},{2,0},{3,1},{4,6},{5,7},{6,4},{7,5},{8,10},{9,11},{10,... | collective-permute-start | bytes 393224 | tf_op jit(solution)/shard_map/ppermute | solution.py:227
  60.3 7.2 %collective-permute-start.7 = (bf16[512,128]{1,0:T(8,128)(2,1)S(1)}, bf16[512,128]{1,0:T(8,128)(2,1)S(1)}, u32[]{:S(2)}, u32[]{:S(2)}) collective-permute-start(bf16[512,128]{1,0:T(8,128)(2,1)S(1)} %get-tuple-element.62.piece), channel_id=1, source_target_pairs={{0,6},{1,7},{2,4},{3,5},{4,2},{5,3},{6,0},{7,1},{8,14},{9,15},{10,... | collective-permute-start | bytes 393224 | tf_op jit(solution)/shard_map/ppermute | solution.py:227
  62.3 7.1 %collective-permute-start.5 = (bf16[512,128]{1,0:T(8,128)(2,1)S(1)}, bf16[512,128]{1,0:T(8,128)(2,1)S(1)}, u32[]{:S(2)}, u32[]{:S(2)}) collective-permute-start(bf16[512,128]{1,0:T(8,128)(2,1)S(1)} %get-tuple-element.62.piece), channel_id=1, source_target_pairs={{0,4},{1,5},{2,6},{3,7},{4,0},{5,1},{6,2},{7,3},{8,12},{9,13},{10,... | collective-permute-start | bytes 393224 | tf_op jit(solution)/shard_map/ppermute | solution.py:227
  65.1 5.1 %collective-permute-start.10 = (bf16[512,128]{1,0:T(8,128)(2,1)S(1)}, bf16[512,128]{1,0:T(8,128)(2,1)S(1)}, u32[]{:S(2)}, u32[]{:S(2)}) collective-permute-start(bf16[512,128]{1,0:T(8,128)(2,1)S(1)} %collective-permute-done.9.refs_0_), channel_id=1, source_target_pairs={{0,1},{1,0},{2,3},{3,2},{4,5},{5,4},{6,7},{7,6},{8,9},{9,8},{10,11... | collective-permute-start | bytes 393224 | tf_op jit(solution)/shard_map/ppermute | solution.py:236
  73.2 5.9 %collective-permute-start.15 = (bf16[512,128]{1,0:T(8,128)(2,1)S(1)}, bf16[512,128]{1,0:T(8,128)(2,1)S(1)}, u32[]{:S(2)}, u32[]{:S(2)}) collective-permute-start(bf16[512,128]{1,0:T(8,128)(2,1)S(1)} %get-tuple-element.69.piece), channel_id=1, source_target_pairs={{0,2},{1,3},{2,0},{3,1},{4,6},{5,7},{6,4},{7,5},{8,10},{9,11},{10,... | collective-permute-start | bytes 393224 | tf_op jit(solution)/shard_map/ppermute | solution.py:227
  73.3 6.5 %collective-permute-start.13 = (bf16[512,128]{1,0:T(8,128)(2,1)S(1)}, bf16[512,128]{1,0:T(8,128)(2,1)S(1)}, u32[]{:S(2)}, u32[]{:S(2)}) collective-permute-start(bf16[512,128]{1,0:T(8,128)(2,1)S(1)} %get-tuple-element.69.piece), channel_id=1, source_target_pairs={{0,6},{1,7},{2,4},{3,5},{4,2},{5,3},{6,0},{7,1},{8,14},{9,15},{10,... | collective-permute-start | bytes 393224 | tf_op jit(solution)/shard_map/ppermute | solution.py:227
  75.3 7.0 %collective-permute-start.11 = (bf16[512,128]{1,0:T(8,128)(2,1)S(1)}, bf16[512,128]{1,0:T(8,128)(2,1)S(1)}, u32[]{:S(2)}, u32[]{:S(2)}) collective-permute-start(bf16[512,128]{1,0:T(8,128)(2,1)S(1)} %get-tuple-element.69.piece), channel_id=1, source_target_pairs={{0,4},{1,5},{2,6},{3,7},{4,0},{5,1},{6,2},{7,3},{8,12},{9,13},{10,... | collective-permute-start | bytes 393224 | tf_op jit(solution)/shard_map/ppermute | solution.py:227
  79.1 4.6 %collective-permute-start.16 = (bf16[512,128]{1,0:T(8,128)(2,1)S(1)}, bf16[512,128]{1,0:T(8,128)(2,1)S(1)}, u32[]{:S(2)}, u32[]{:S(2)}) collective-permute-start(bf16[512,128]{1,0:T(8,128)(2,1)S(1)} %collective-permute-done.15.near), channel_id=1, source_target_pairs={{0,1},{1,0},{2,3},{3,2},{4,5},{5,4},{6,7},{7,6},{8,9},{9,8},{10,11... | collective-permute-start | bytes 393224 | tf_op jit(solution)/shard_map/ppermute | solution.py:236
  79.8 4.7 %collective-permute-start.14 = (bf16[512,128]{1,0:T(8,128)(2,1)S(1)}, bf16[512,128]{1,0:T(8,128)(2,1)S(1)}, u32[]{:S(2)}, u32[]{:S(2)}) collective-permute-start(bf16[512,128]{1,0:T(8,128)(2,1)S(1)} %collective-permute-done.13.refs_2_), channel_id=1, source_target_pairs={{0,1},{1,0},{2,3},{3,2},{4,5},{5,4},{6,7},{7,6},{8,9},{9,8},{10,11... | collective-permute-start | bytes 393224 | tf_op jit(solution)/shard_map/ppermute | solution.py:236
  112.0 5.8 %collective-permute-start.22 = (bf16[512,128]{1,0:T(8,128)(2,1)S(1)}, bf16[512,128]{1,0:T(8,128)(2,1)S(1)}, u32[]{:S(2)}, u32[]{:S(2)}) collective-permute-start(bf16[512,128]{1,0:T(8,128)(2,1)S(1)} %get-tuple-element.78.piece), channel_id=1, source_target_pairs={{0,2},{1,3},{2,0},{3,1},{4,6},{5,7},{6,4},{7,5},{8,10},{9,11},{10,... | collective-permute-start | bytes 393224 | tf_op jit(solution)/shard_map/ppermute | solution.py:227
  112.1 6.4 %collective-permute-start.20 = (bf16[512,128]{1,0:T(8,128)(2,1)S(1)}, bf16[512,128]{1,0:T(8,128)(2,1)S(1)}, u32[]{:S(2)}, u32[]{:S(2)}) collective-permute-start(bf16[512,128]{1,0:T(8,128)(2,1)S(1)} %get-tuple-element.78.piece), channel_id=1, source_target_pairs={{0,6},{1,7},{2,4},{3,5},{4,2},{5,3},{6,0},{7,1},{8,14},{9,15},{10,... | collective-permute-start | bytes 393224 | tf_op jit(solution)/shard_map/ppermute | solution.py:227
  113.9 7.4 %collective-permute-start.18 = (bf16[512,128]{1,0:T(8,128)(2,1)S(1)}, bf16[512,128]{1,0:T(8,128)(2,1)S(1)}, u32[]{:S(2)}, u32[]{:S(2)}) collective-permute-start(bf16[512,128]{1,0:T(8,128)(2,1)S(1)} %get-tuple-element.78.piece), channel_id=1, source_target_pairs={{0,4},{1,5},{2,6},{3,7},{4,0},{5,1},{6,2},{7,3},{8,12},{9,13},{10,... | collective-permute-start | bytes 393224 | tf_op jit(solution)/shard_map/ppermute | solution.py:227
  117.8 4.5 %collective-permute-start.23 = (bf16[512,128]{1,0:T(8,128)(2,1)S(1)}, bf16[512,128]{1,0:T(8,128)(2,1)S(1)}, u32[]{:S(2)}, u32[]{:S(2)}) collective-permute-start(bf16[512,128]{1,0:T(8,128)(2,1)S(1)} %collective-permute-done.22.refs_0_), channel_id=1, source_target_pairs={{0,1},{1,0},{2,3},{3,2},{4,5},{5,4},{6,7},{7,6},{8,9},{9,8},{10,11... | collective-permute-start | bytes 393224 | tf_op jit(solution)/shard_map/ppermute | solution.py:236
  118.4 5.2 %collective-permute-start.21 = (bf16[512,128]{1,0:T(8,128)(2,1)S(1)}, bf16[512,128]{1,0:T(8,128)(2,1)S(1)}, u32[]{:S(2)}, u32[]{:S(2)}) collective-permute-start(bf16[512,128]{1,0:T(8,128)(2,1)S(1)} %collective-permute-done.20.refs_2_), channel_id=1, source_target_pairs={{0,1},{1,0},{2,3},{3,2},{4,5},{5,4},{6,7},{7,6},{8,9},{9,8},{10,11... | collective-permute-start | bytes 393224 | tf_op jit(solution)/shard_map/ppermute | solution.py:236
  125.2 5.8 %collective-permute-start.28 = (bf16[512,128]{1,0:T(8,128)(2,1)S(1)}, bf16[512,128]{1,0:T(8,128)(2,1)S(1)}, u32[]{:S(2)}, u32[]{:S(2)}) collective-permute-start(bf16[512,128]{1,0:T(8,128)(2,1)S(1)} %get-tuple-element.85.piece), channel_id=1, source_target_pairs={{0,2},{1,3},{2,0},{3,1},{4,6},{5,7},{6,4},{7,5},{8,10},{9,11},{10,... | collective-permute-start | bytes 393224 | tf_op jit(solution)/shard_map/ppermute | solution.py:227
  125.3 6.4 %collective-permute-start.26 = (bf16[512,128]{1,0:T(8,128)(2,1)S(1)}, bf16[512,128]{1,0:T(8,128)(2,1)S(1)}, u32[]{:S(2)}, u32[]{:S(2)}) collective-permute-start(bf16[512,128]{1,0:T(8,128)(2,1)S(1)} %get-tuple-element.85.piece), channel_id=1, source_target_pairs={{0,6},{1,7},{2,4},{3,5},{4,2},{5,3},{6,0},{7,1},{8,14},{9,15},{10,... | collective-permute-start | bytes 393224 | tf_op jit(solution)/shard_map/ppermute | solution.py:227
  127.0 7.0 %collective-permute-start.24 = (bf16[512,128]{1,0:T(8,128)(2,1)S(1)}, bf16[512,128]{1,0:T(8,128)(2,1)S(1)}, u32[]{:S(2)}, u32[]{:S(2)}) collective-permute-start(bf16[512,128]{1,0:T(8,128)(2,1)S(1)} %get-tuple-element.85.piece), channel_id=1, source_target_pairs={{0,4},{1,5},{2,6},{3,7},{4,0},{5,1},{6,2},{7,3},{8,12},{9,13},{10,... | collective-permute-start | bytes 393224 | tf_op jit(solution)/shard_map/ppermute | solution.py:227
  131.0 4.4 %collective-permute-start.29 = (bf16[512,128]{1,0:T(8,128)(2,1)S(1)}, bf16[512,128]{1,0:T(8,128)(2,1)S(1)}, u32[]{:S(2)}, u32[]{:S(2)}) collective-permute-start(bf16[512,128]{1,0:T(8,128)(2,1)S(1)} %collective-permute-done.28.near), channel_id=1, source_target_pairs={{0,1},{1,0},{2,3},{3,2},{4,5},{5,4},{6,7},{7,6},{8,9},{9,8},{10,11... | collective-permute-start | bytes 393224 | tf_op jit(solution)/shard_map/ppermute | solution.py:236
  131.6 4.5 %collective-permute-start.27 = (bf16[512,128]{1,0:T(8,128)(2,1)S(1)}, bf16[512,128]{1,0:T(8,128)(2,1)S(1)}, u32[]{:S(2)}, u32[]{:S(2)}) collective-permute-start(bf16[512,128]{1,0:T(8,128)(2,1)S(1)} %collective-permute-done.26.refs_2_), channel_id=1, source_target_pairs={{0,1},{1,0},{2,3},{3,2},{4,5},{5,4},{6,7},{7,6},{8,9},{9,8},{10,11... | collective-permute-start | bytes 393224 | tf_op jit(solution)/shard_map/ppermute | solution.py:236
  163.6 5.8 %collective-permute-start.35 = (bf16[512,128]{1,0:T(8,128)(2,1)S(1)}, bf16[512,128]{1,0:T(8,128)(2,1)S(1)}, u32[]{:S(2)}, u32[]{:S(2)}) collective-permute-start(bf16[512,128]{1,0:T(8,128)(2,1)S(1)} %get-tuple-element.94.piece), channel_id=1, source_target_pairs={{0,2},{1,3},{2,0},{3,1},{4,6},{5,7},{6,4},{7,5},{8,10},{9,11},{10,... | collective-permute-start | bytes 393224 | tf_op jit(solution)/shard_map/ppermute | solution.py:227
  164.0 6.1 %collective-permute-start.33 = (bf16[512,128]{1,0:T(8,128)(2,1)S(1)}, bf16[512,128]{1,0:T(8,128)(2,1)S(1)}, u32[]{:S(2)}, u32[]{:S(2)}) collective-permute-start(bf16[512,128]{1,0:T(8,128)(2,1)S(1)} %get-tuple-element.94.piece), channel_id=1, source_target_pairs={{0,6},{1,7},{2,4},{3,5},{4,2},{5,3},{6,0},{7,1},{8,14},{9,15},{10,... | collective-permute-start | bytes 393224 | tf_op jit(solution)/shard_map/ppermute | solution.py:227
  165.6 7.4 %collective-permute-start.31 = (bf16[512,128]{1,0:T(8,128)(2,1)S(1)}, bf16[512,128]{1,0:T(8,128)(2,1)S(1)}, u32[]{:S(2)}, u32[]{:S(2)}) collective-permute-start(bf16[512,128]{1,0:T(8,128)(2,1)S(1)} %get-tuple-element.94.piece), channel_id=1, source_target_pairs={{0,4},{1,5},{2,6},{3,7},{4,0},{5,1},{6,2},{7,3},{8,12},{9,13},{10,... | collective-permute-start | bytes 393224 | tf_op jit(solution)/shard_map/ppermute | solution.py:227
  169.4 4.5 %collective-permute-start.36 = (bf16[512,128]{1,0:T(8,128)(2,1)S(1)}, bf16[512,128]{1,0:T(8,128)(2,1)S(1)}, u32[]{:S(2)}, u32[]{:S(2)}) collective-permute-start(bf16[512,128]{1,0:T(8,128)(2,1)S(1)} %collective-permute-done.35.refs_0_), channel_id=1, source_target_pairs={{0,1},{1,0},{2,3},{3,2},{4,5},{5,4},{6,7},{7,6},{8,9},{9,8},{10,11... | collective-permute-start | bytes 393224 | tf_op jit(solution)/shard_map/ppermute | solution.py:236
  170.0 5.3 %collective-permute-start.34 = (bf16[512,128]{1,0:T(8,128)(2,1)S(1)}, bf16[512,128]{1,0:T(8,128)(2,1)S(1)}, u32[]{:S(2)}, u32[]{:S(2)}) collective-permute-start(bf16[512,128]{1,0:T(8,128)(2,1)S(1)} %collective-permute-done.33.refs_2_), channel_id=1, source_target_pairs={{0,1},{1,0},{2,3},{3,2},{4,5},{5,4},{6,7},{7,6},{8,9},{9,8},{10,11... | collective-permute-start | bytes 393224 | tf_op jit(solution)/shard_map/ppermute | solution.py:236
  176.9 5.8 %collective-permute-start.41 = (bf16[512,128]{1,0:T(8,128)(2,1)S(1)}, bf16[512,128]{1,0:T(8,128)(2,1)S(1)}, u32[]{:S(2)}, u32[]{:S(2)}) collective-permute-start(bf16[512,128]{1,0:T(8,128)(2,1)S(1)} %get-tuple-element.102.refs_3_), channel_id=1, source_target_pairs={{0,2},{1,3},{2,0},{3,1},{4,6},{5,7},{6,4},{7,5},{8,10},{9,11},{10,... | collective-permute-start | bytes 393224 | tf_op jit(solution)/shard_map/ppermute | solution.py:227
  177.0 6.4 %collective-permute-start.39 = (bf16[512,128]{1,0:T(8,128)(2,1)S(1)}, bf16[512,128]{1,0:T(8,128)(2,1)S(1)}, u32[]{:S(2)}, u32[]{:S(2)}) collective-permute-start(bf16[512,128]{1,0:T(8,128)(2,1)S(1)} %get-tuple-element.102.refs_3_), channel_id=1, source_target_pairs={{0,6},{1,7},{2,4},{3,5},{4,2},{5,3},{6,0},{7,1},{8,14},{9,15},{10,... | collective-permute-start | bytes 393224 | tf_op jit(solution)/shard_map/ppermute | solution.py:227
  178.6 7.0 %collective-permute-start.37 = (bf16[512,128]{1,0:T(8,128)(2,1)S(1)}, bf16[512,128]{1,0:T(8,128)(2,1)S(1)}, u32[]{:S(2)}, u32[]{:S(2)}) collective-permute-start(bf16[512,128]{1,0:T(8,128)(2,1)S(1)} %get-tuple-element.102.refs_3_), channel_id=1, source_target_pairs={{0,4},{1,5},{2,6},{3,7},{4,0},{5,1},{6,2},{7,3},{8,12},{9,13},{10,... | collective-permute-start | bytes 393224 | tf_op jit(solution)/shard_map/ppermute | solution.py:227
  183.3 4.5 %collective-permute-start.40 = (bf16[512,128]{1,0:T(8,128)(2,1)S(1)}, bf16[512,128]{1,0:T(8,128)(2,1)S(1)}, u32[]{:S(2)}, u32[]{:S(2)}) collective-permute-start(bf16[512,128]{1,0:T(8,128)(2,1)S(1)} %collective-permute-done.39.refs_5_), channel_id=1, source_target_pairs={{0,1},{1,0},{2,3},{3,2},{4,5},{5,4},{6,7},{7,6},{8,9},{9,8},{10,11... | collective-permute-start | bytes 393224 | tf_op jit(solution)/shard_map/ppermute | solution.py:236
  (22 other events, 77.3 us)

commit v2 on v1

--- a/solution.py
+++ b/solution.py
@@ -16,6 +16,7 @@
 
 VMEM = pl.BlockSpec(memory_space=pltpu.VMEM)
 SMEM = pl.BlockSpec(memory_space=pltpu.SMEM)
+HBM = pl.BlockSpec(memory_space=pltpu.HBM)
 F32 = jnp.float32
 BF16 = jnp.bfloat16
 
@@ -178,8 +179,17 @@
     return jnp.transpose(jnp.broadcast_to(row, (BLOCK, row.shape[1])))
 
 
-def drive_kernel(weight, stimulus, bias, leak, local_weight, out, leak_out):
-    del local_weight
+def fetch(sources, places, done):
+    copies = [pltpu.make_async_copy(x, y, done.at[i]) for i, (x, y) in enumerate(zip(sources, places))]
+    for copy in copies:
+        copy.start()
+    for copy in copies:
+        copy.wait()
+
+
+def drive_kernel(*refs):
+    out, leak_out, weight, stimulus, bias, leak, done = refs[-7:]
+    fetch(refs[:4], (weight, stimulus, bias, leak), done)
     leak_out[...] = column(leak[...])
     base = column(bias[...])
 
@@ -191,22 +201,22 @@
     lax.fori_loop(0, 2 * WINDOWS, one, 0)
 
 
-def both_kernel(rates, prior, out):
-    out[0:ROWS, :] = rates[...].astype(BF16)
-    out[ROWS : 2 * ROWS, :] = prior[...]
-
-
-def call(kernel, inputs, outs, flops, scratch=(), aliases=None):
+def both_kernel(rates, prior, out, rates_here, done):
+    fetch((rates, prior), (rates_here, out.at[ROWS : 2 * ROWS, :]), done)
+    out[0:ROWS, :] = rates_here[...].astype(BF16)
+
+
+def call(kernel, inputs, outs, flops, scratch=(), aliases=None, far=0):
     byte_count = sum(x.size * x.dtype.itemsize for x in inputs)
     return pl.pallas_call(
         kernel,
         out_shape=outs,
-        in_specs=[SMEM if x.dtype == jnp.int32 else VMEM for x in inputs],
+        in_specs=[HBM if i < far else SMEM if x.dtype == jnp.int32 else VMEM for i, x in enumerate(inputs)],
         out_specs=jax.tree.map(lambda _: VMEM, outs),
         scratch_shapes=list(scratch),
         input_output_aliases=aliases or {},
         cost_estimate=pl.CostEstimate(flops=flops, bytes_accessed=byte_count, transcendentals=0),
-        compiler_params=pltpu.CompilerParams(vmem_limit_bytes=24 * 2**20),
+        compiler_params=pltpu.CompilerParams(vmem_limit_bytes=None if far else 24 * 2**20),
     )(*inputs)
 
 
@@ -273,11 +283,14 @@
     tables = [table, lists, counts]
     weight_local = local_weight[0]
     weight_long = long_weight[0]
+    inputs = [input_weight[0].T, stimulus, unit_bias, leak_rate]
     drives, leak = call(
         drive_kernel,
-        [input_weight[0].T, stimulus, unit_bias, leak_rate, weight_local],
+        inputs,
         (jax.ShapeDtypeStruct((2 * WINDOWS, ROWS, BLOCK), F32), shape(ROWS, F32)),
         1000,
+        [*(pltpu.VMEM(x.shape, x.dtype) for x in inputs[:4]), pltpu.SemaphoreType.DMA((4,))],
+        far=4,
     )
     flops = ROWS * UNITS * BLOCK
 
@@ -290,7 +303,14 @@
     history = shape(UNITS, BF16)
     parcels = jax.ShapeDtypeStruct((BLOCKS, HALF, BLOCK), BF16)
     half_history = shape(UNITS // 2, BF16)
-    both = call(both_kernel, [initial_rates[0], prior_rates[0]], shape(2 * ROWS, BF16), 1000)
+    both = call(
+        both_kernel,
+        [initial_rates[0], prior_rates[0]],
+        shape(2 * ROWS, BF16),
+        1000,
+        [pltpu.VMEM((ROWS, BLOCK), F32), pltpu.SemaphoreType.DMA((2,))],
+        far=2,
+    )
     near, second, far = neighbours(both)
     own = paired(both)
     far, drives, leak = lax.optimization_barrier((far, drives, leak))

time: 216 us -> 215 us (level)
  local copies, waits for them, and re-layouts: 7.86 us -> 1.01 us
  Pallas kernels: 28.6 us -> 32.3 us
    unnamed x20 -> x10, local copies, waits for them, and re-layouts: 6.87 us -> 0.03 us
    pallas_call x23, Pallas kernels: 28.6 us -> 32.3 us  [call(): pl.pallas_call(kernel, out_shape=outs, in_specs=[HBM if i < far else SMEM...]
  transfers between devices with their start and end apart: 44 -> 44, of which waited for: 12 -> 11; matrix products, arithmetic and copies ran while one was open for 1% -> 1% of each run, Pallas kernels for 7% -> 8%
where the time goes in v2:
time: 215 us; the launch traced here: 214 us
  blocking collectives  116 us (54%)
  starting transfers between devices  55 us (26%)
  Pallas kernels  32.3 us (15%)
  waiting for transfers between devices  6.84 us (3%)
    all_to_all x4, blocking collectives, long_range(): lax.all_to_all(outgoing, 'area', split_axis=0, concat_axis=0, tiled=True)  91.4 us
    pallas_call x23, Pallas kernels, call(): pl.pallas_call(kernel, out_shape=outs, in_specs=[HBM if i < far else SMEM...  32.3 us
    ppermute x21, starting transfers between devices, neighbours(): found.append(lax.ppermute(piece, 'unit', [(u, u ^ m) for u in range(8)]))  24.9 us
    all_gather x9, blocking collectives, paired(): lax.all_gather(piece, 'unit', axis=0, tiled=True, axis_index_groups=[[0,...  24.7 us
    ppermute x18, starting transfers between devices, exchange(): pieces += [x, lax.ppermute(x, 'unit', PAIRS)]  21.7 us
    ppermute x4, starting transfers between devices, long_range(): other = lax.ppermute(arrived, 'unit', PAIRS)  7.98 us
    ppermute x21, waiting for transfers between devices, neighbours(): found.append(lax.ppermute(piece, 'unit', [(u, u ^ m) for u in range(8)]))  5.06 us
  transfers between devices with their start and end apart: 44, of which 11 were waited for; matrix products, arithmetic and copies ran while one was open for 1% of the time, Pallas kernels for 8%

profile of v2, /device:TPU:1, one launch (start us, length us, event | category | flops | bytes accessed | tf_op | source)
XLA Modules:
  0.0 214.2 jit_solution(18125803097937245371)
XLA Ops:
  0.6 1.7 shard_map.122
  2.4 3.6 %collective-permute-start.3 = (bf16[1024,128]{1,0:T(8,128)(2,1)}, bf16[1024,128]{1,0:T(8,128)(2,1)S(1)}, u32[]{:S(2)}, u32[]{:S(2)}) collective-permute-start(bf16[1024,128]{1,0:T(8,128)(2,1)} %shard_map.122), channel_id=1, source_target_pairs={{0,6},{1,7},{2,4},{3,5},{4,2},{5,3},{6,0},{7,1},{8,14},{9,15},{10,... | collective-permute-start | bytes 786440 | tf_op jit(solution)/shard_map/ppermute | solution.py:237
  9.4 3.6 %shard_map.123 = (f32[6,512,128]{2,1,0:T(8,128)}, f32[512,128]{1,0:T(8,128)}) custom-call(bf16[16,512]{1,0:T(8,128)(2,1)} %bitcast.39, bf16[6,16,128]{2,1,0:T(8,128)(2,1)} %refs_1_.1, f32[1,512]{1,0:T(1,128)} %refs_2_.1, f32[1,512]{1,0:T(1,128)} %refs_3_.1), custom_call_target="tpu_custom_call" | custom-call | flops 1000 | bytes 45056 | tf_op jit(solution)/shard_map/pallas_call | solution.py:211
  13.0 5.1 %all_gather.27.own = bf16[2048,128]{1,0:T(8,128)(2,1)S(1)} all-gather(bf16[1024,128]{1,0:T(8,128)(2,1)} %shard_map.122), channel_id=1, replica_groups={{0,1},{2,3},{4,5},{6,7},{8,9},{10,11},{12,13},{14,15},{16,17},{18,19},{..., dimensions={0}, use_global_device_ids=true | all-gather | bytes 786432 | tf_op jit(solution)/shard_map/all_gather | solution.py:228
  18.5 2.4 %all_gather.29.second = bf16[2048,128]{1,0:T(8,128)(2,1)S(1)} all-gather(bf16[1024,128]{1,0:T(8,128)(2,1)S(1)} %collective-permute-done.3), channel_id=1, replica_groups={{0,1},{2,3},{4,5},{6,7},{8,9},{10,11},{12,13},{14,15},{16,17},{18,19},{..., dimensions={0}, use_global_device_ids=true | all-gather | bytes 786432 | tf_op jit(solution)/shard_map/all_gather | solution.py:228
  20.9 2.3 %all_gather.28.near = bf16[2048,128]{1,0:T(8,128)(2,1)S(1)} all-gather(bf16[1024,128]{1,0:T(8,128)(2,1)S(1)} %collective-permute-done), channel_id=1, replica_groups={{0,1},{2,3},{4,5},{6,7},{8,9},{10,11},{12,13},{14,15},{16,17},{18,19},{..., dimensions={0}, use_global_device_ids=true | all-gather | bytes 786432 | tf_op jit(solution)/shard_map/all_gather | solution.py:228
  24.1 28.2 %all_to_all.20.mine = bf16[32,64,128]{2,1,0:T(8,128)(2,1)S(1)} all-to-all(bf16[32,64,128]{2,1,0:T(8,128)(2,1)S(1)} %get-tuple-element.57), channel_id=1, replica_groups=mesh['area'=32,'unit'=8] {'area'}, dimensions={0} | all-to-all | bytes 1048576 | tf_op jit(solution)/shard_map/all_to_all | solution.py:298
  52.4 2.1 %collective-permute-start.4 = (bf16[32,64,128]{2,1,0:T(8,128)(2,1)S(1)}, bf16[32,64,128]{2,1,0:T(8,128)(2,1)S(1)}, u32[]{:S(2)}, u32[]{:S(2)}) collective-permute-start(bf16[32,64,128]{2,1,0:T(8,128)(2,1)S(1)} %all_to_all.20.mine), channel_id=1, source_target_pairs={{0,1},{1,0},{2,3},{3,2},{4,5},{5,4},{6,7},{7,6},{8,9},{9,8},{10,11... | collective-permute-start | bytes 1572872 | tf_op jit(solution)/shard_map/ppermute | solution.py:299
  54.7 1.9 shard_map.125.partial
  58.3 2.8 %collective-permute-start.7 = (bf16[512,128]{1,0:T(8,128)(2,1)S(1)}, bf16[512,128]{1,0:T(8,128)(2,1)S(1)}, u32[]{:S(2)}, u32[]{:S(2)}) collective-permute-start(bf16[512,128]{1,0:T(8,128)(2,1)S(1)} %get-tuple-element.62.piece), channel_id=1, source_target_pairs={{0,6},{1,7},{2,4},{3,5},{4,2},{5,3},{6,0},{7,1},{8,14},{9,15},{10,... | collective-permute-start | bytes 393224 | tf_op jit(solution)/shard_map/ppermute | solution.py:237
  62.1 2.2 %all_gather.30.pair = bf16[1024,128]{1,0:T(8,128)(2,1)S(1)} all-gather(bf16[512,128]{1,0:T(8,128)(2,1)S(1)} %get-tuple-element.62.piece), channel_id=1, replica_groups={{0,1},{2,3},{4,5},{6,7},{8,9},{10,11},{12,13},{14,15},{16,17},{18,19},{..., dimensions={0}, use_global_device_ids=true | all-gather | bytes 393216 | tf_op jit(solution)/shard_map/all_gather | solution.py:228
  64.6 1.9 collective-permute-done.7.refs_2_
  72.4 1.7 collective-permute-start.13
  75.6 2.5 %all_gather.31.pair = bf16[1024,128]{1,0:T(8,128)(2,1)S(1)} all-gather(bf16[512,128]{1,0:T(8,128)(2,1)S(1)} %get-tuple-element.69.piece), channel_id=1, replica_groups={{0,1},{2,3},{4,5},{6,7},{8,9},{10,11},{12,13},{14,15},{16,17},{18,19},{..., dimensions={0}, use_global_device_ids=true | all-gather | bytes 393216 | tf_op jit(solution)/shard_map/all_gather | solution.py:228
  84.0 21.2 %all_to_all.21.mine = bf16[32,64,128]{2,1,0:T(8,128)(2,1)S(1)} all-to-all(bf16[32,64,128]{2,1,0:T(8,128)(2,1)S(1)} %get-tuple-element.74), channel_id=1, replica_groups=mesh['area'=32,'unit'=8] {'area'}, dimensions={0} | all-to-all | bytes 1048576 | tf_op jit(solution)/shard_map/all_to_all | solution.py:298
  105.2 1.9 collective-permute-start.17
  107.2 1.9 shard_map.131.partial
  114.0 2.5 %all_gather.32.pair = bf16[1024,128]{1,0:T(8,128)(2,1)S(1)} all-gather(bf16[512,128]{1,0:T(8,128)(2,1)S(1)} %get-tuple-element.78.piece), channel_id=1, replica_groups={{0,1},{2,3},{4,5},{6,7},{8,9},{10,11},{12,13},{14,15},{16,17},{18,19},{..., dimensions={0}, use_global_device_ids=true | all-gather | bytes 393216 | tf_op jit(solution)/shard_map/all_gather | solution.py:228
  117.1 2.1 collective-permute-start.21
  124.1 1.7 collective-permute-start.26
  127.3 2.5 %all_gather.33.pair = bf16[1024,128]{1,0:T(8,128)(2,1)S(1)} all-gather(bf16[512,128]{1,0:T(8,128)(2,1)S(1)} %get-tuple-element.85.piece), channel_id=1, replica_groups={{0,1},{2,3},{4,5},{6,7},{8,9},{10,11},{12,13},{14,15},{16,17},{18,19},{..., dimensions={0}, use_global_device_ids=true | all-gather | bytes 393216 | tf_op jit(solution)/shard_map/all_gather | solution.py:228
  130.4 1.9 collective-permute-start.27
  135.7 21.2 %all_to_all.22.mine = bf16[32,64,128]{2,1,0:T(8,128)(2,1)S(1)} all-to-all(bf16[32,64,128]{2,1,0:T(8,128)(2,1)S(1)} %get-tuple-element.90), channel_id=1, replica_groups=mesh['area'=32,'unit'=8] {'area'}, dimensions={0} | all-to-all | bytes 1048576 | tf_op jit(solution)/shard_map/all_to_all | solution.py:298
  156.9 1.9 collective-permute-start.30
  158.8 1.9 shard_map.137.partial
  165.6 2.5 %all_gather.34.pair = bf16[1024,128]{1,0:T(8,128)(2,1)S(1)} all-gather(bf16[512,128]{1,0:T(8,128)(2,1)S(1)} %get-tuple-element.94.piece), channel_id=1, replica_groups={{0,1},{2,3},{4,5},{6,7},{8,9},{10,11},{12,13},{14,15},{16,17},{18,19},{..., dimensions={0}, use_global_device_ids=true | all-gather | bytes 393216 | tf_op jit(solution)/shard_map/all_gather | solution.py:228
  168.8 3.9 %collective-permute-start.34 = (bf16[512,128]{1,0:T(8,128)(2,1)S(1)}, bf16[512,128]{1,0:T(8,128)(2,1)S(1)}, u32[]{:S(2)}, u32[]{:S(2)}) collective-permute-start(bf16[512,128]{1,0:T(8,128)(2,1)S(1)} %collective-permute-done.33.refs_2_), channel_id=1, source_target_pairs={{0,1},{1,0},{2,3},{3,2},{4,5},{5,4},{6,7},{7,6},{8,9},{9,8},{10,11... | collective-permute-start | bytes 393224 | tf_op jit(solution)/shard_map/ppermute | solution.py:246
  179.0 3.0 %all_gather.35.refs_4_ = bf16[1024,128]{1,0:T(8,128)(2,1)S(1)} all-gather(bf16[512,128]{1,0:T(8,128)(2,1)S(1)} %get-tuple-element.102.refs_3_), channel_id=1, replica_groups={{0,1},{2,3},{4,5},{6,7},{8,9},{10,11},{12,13},{14,15},{16,17},{18,19},{..., dimensions={0}, use_global_device_ids=true | all-gather | bytes 393216 | tf_op jit(solution)/shard_map/all_gather | solution.py:228
  182.6 3.2 %collective-permute-start.40 = (bf16[512,128]{1,0:T(8,128)(2,1)S(1)}, bf16[512,128]{1,0:T(8,128)(2,1)S(1)}, u32[]{:S(2)}, u32[]{:S(2)}) collective-permute-start(bf16[512,128]{1,0:T(8,128)(2,1)S(1)} %collective-permute-done.39.refs_5_), channel_id=1, source_target_pairs={{0,1},{1,0},{2,3},{3,2},{4,5},{5,4},{6,7},{7,6},{8,9},{9,8},{10,11... | collective-permute-start | bytes 393224 | tf_op jit(solution)/shard_map/ppermute | solution.py:246
  187.7 20.8 %all_to_all.23.mine = bf16[32,64,128]{2,1,0:T(8,128)(2,1)S(1)} all-to-all(bf16[32,64,128]{2,1,0:T(8,128)(2,1)S(1)} %shard_map.143), channel_id=1, replica_groups=mesh['area'=32,'unit'=8] {'area'}, dimensions={0} | all-to-all | bytes 1048576 | tf_op jit(solution)/shard_map/all_to_all | solution.py:298
  208.5 1.9 collective-permute-start.43
  212.0 2.2 %shard_map.144 = f32[512,128]{1,0:T(8,128)} custom-call(s32[64]{0:T(128)S(1)} %pad_add_fusion.table.refs_0_, bf16[512,2048]{1,0:T(8,128)(2,1)S(1)} %bitcast.33, bf16[32,64,128]{2,1,0:T(8,128)(2,1)S(1)} %all_to_all.23.mine, bf16[32,64,128]{2,1,0:T(8,128)(2,1)S(1)} %collective-permute-done.43.theirs), custom_call_target="tpu_custom_call" | custom-call | flops 268435456 | bytes 3145984 | tf_op jit(solution)/shard_map/pallas_call | solution.py:211
  (114 shorter events, 53.0 us)
Async XLA Ops:
  2.4 16.1 %collective-permute-start.3 = (bf16[1024,128]{1,0:T(8,128)(2,1)}, bf16[1024,128]{1,0:T(8,128)(2,1)S(1)}, u32[]{:S(2)}, u32[]{:S(2)}) collective-permute-start(bf16[1024,128]{1,0:T(8,128)(2,1)} %shard_map.122), channel_id=1, source_target_pairs={{0,6},{1,7},{2,4},{3,5},{4,2},{5,3},{6,0},{7,1},{8,14},{9,15},{10,... | collective-permute-start | bytes 786440 | tf_op jit(solution)/shard_map/ppermute | solution.py:237
  6.0 12.1 %collective-permute-start.1 = (bf16[1024,128]{1,0:T(8,128)(2,1)}, bf16[1024,128]{1,0:T(8,128)(2,1)S(1)}, u32[]{:S(2)}, u32[]{:S(2)}) collective-permute-start(bf16[1024,128]{1,0:T(8,128)(2,1)} %shard_map.122), channel_id=1, source_target_pairs={{0,4},{1,5},{2,6},{3,7},{4,0},{5,1},{6,2},{7,3},{8,12},{9,13},{10,... | collective-permute-start | bytes 786440 | tf_op jit(solution)/shard_map/ppermute | solution.py:237
  6.3 14.5 %collective-permute-start = (bf16[1024,128]{1,0:T(8,128)(2,1)}, bf16[1024,128]{1,0:T(8,128)(2,1)S(1)}, u32[]{:S(2)}, u32[]{:S(2)}) collective-permute-start(bf16[1024,128]{1,0:T(8,128)(2,1)} %shard_map.122), channel_id=1, source_target_pairs={{0,2},{1,3},{2,0},{3,1},{4,6},{5,7},{6,4},{7,5},{8,10},{9,11},{10,... | collective-permute-start | bytes 786440 | tf_op jit(solution)/shard_map/ppermute | solution.py:237
  18.1 5.1 %collective-permute-start.2 = (bf16[1024,128]{1,0:T(8,128)(2,1)S(1)}, bf16[1024,128]{1,0:T(8,128)(2,1)S(1)}, u32[]{:S(2)}, u32[]{:S(2)}) collective-permute-start(bf16[1024,128]{1,0:T(8,128)(2,1)S(1)} %collective-permute-done.1.far), channel_id=1, source_target_pairs={{0,1},{1,0},{2,3},{3,2},{4,5},{5,4},{6,7},{7,6},{8,9},{9,8},{10,11... | collective-permute-start | bytes 786440 | tf_op jit(solution)/shard_map/ppermute | solution.py:318
  52.4 4.3 %collective-permute-start.4 = (bf16[32,64,128]{2,1,0:T(8,128)(2,1)S(1)}, bf16[32,64,128]{2,1,0:T(8,128)(2,1)S(1)}, u32[]{:S(2)}, u32[]{:S(2)}) collective-permute-start(bf16[32,64,128]{2,1,0:T(8,128)(2,1)S(1)} %all_to_all.20.mine), channel_id=1, source_target_pairs={{0,1},{1,0},{2,3},{3,2},{4,5},{5,4},{6,7},{7,6},{8,9},{9,8},{10,11... | collective-permute-start | bytes 1572872 | tf_op jit(solution)/shard_map/ppermute | solution.py:299
  58.1 6.1 %collective-permute-start.9 = (bf16[512,128]{1,0:T(8,128)(2,1)S(1)}, bf16[512,128]{1,0:T(8,128)(2,1)S(1)}, u32[]{:S(2)}, u32[]{:S(2)}) collective-permute-start(bf16[512,128]{1,0:T(8,128)(2,1)S(1)} %get-tuple-element.62.piece), channel_id=1, source_target_pairs={{0,2},{1,3},{2,0},{3,1},{4,6},{5,7},{6,4},{7,5},{8,10},{9,11},{10,... | collective-permute-start | bytes 393224 | tf_op jit(solution)/shard_map/ppermute | solution.py:237
  58.3 8.3 %collective-permute-start.7 = (bf16[512,128]{1,0:T(8,128)(2,1)S(1)}, bf16[512,128]{1,0:T(8,128)(2,1)S(1)}, u32[]{:S(2)}, u32[]{:S(2)}) collective-permute-start(bf16[512,128]{1,0:T(8,128)(2,1)S(1)} %get-tuple-element.62.piece), channel_id=1, source_target_pairs={{0,6},{1,7},{2,4},{3,5},{4,2},{5,3},{6,0},{7,1},{8,14},{9,15},{10,... | collective-permute-start | bytes 393224 | tf_op jit(solution)/shard_map/ppermute | solution.py:237
  61.0 7.5 %collective-permute-start.5 = (bf16[512,128]{1,0:T(8,128)(2,1)S(1)}, bf16[512,128]{1,0:T(8,128)(2,1)S(1)}, u32[]{:S(2)}, u32[]{:S(2)}) collective-permute-start(bf16[512,128]{1,0:T(8,128)(2,1)S(1)} %get-tuple-element.62.piece), channel_id=1, source_target_pairs={{0,4},{1,5},{2,6},{3,7},{4,0},{5,1},{6,2},{7,3},{8,12},{9,13},{10,... | collective-permute-start | bytes 393224 | tf_op jit(solution)/shard_map/ppermute | solution.py:237
  64.3 5.1 %collective-permute-start.10 = (bf16[512,128]{1,0:T(8,128)(2,1)S(1)}, bf16[512,128]{1,0:T(8,128)(2,1)S(1)}, u32[]{:S(2)}, u32[]{:S(2)}) collective-permute-start(bf16[512,128]{1,0:T(8,128)(2,1)S(1)} %collective-permute-done.9.refs_0_), channel_id=1, source_target_pairs={{0,1},{1,0},{2,3},{3,2},{4,5},{5,4},{6,7},{7,6},{8,9},{9,8},{10,11... | collective-permute-start | bytes 393224 | tf_op jit(solution)/shard_map/ppermute | solution.py:246
  66.5 4.2 %collective-permute-start.8 = (bf16[512,128]{1,0:T(8,128)(2,1)S(1)}, bf16[512,128]{1,0:T(8,128)(2,1)S(1)}, u32[]{:S(2)}, u32[]{:S(2)}) collective-permute-start(bf16[512,128]{1,0:T(8,128)(2,1)S(1)} %collective-permute-done.7.refs_2_), channel_id=1, source_target_pairs={{0,1},{1,0},{2,3},{3,2},{4,5},{5,4},{6,7},{7,6},{8,9},{9,8},{10,11... | collective-permute-start | bytes 393224 | tf_op jit(solution)/shard_map/ppermute | solution.py:246
  72.3 5.8 %collective-permute-start.15 = (bf16[512,128]{1,0:T(8,128)(2,1)S(1)}, bf16[512,128]{1,0:T(8,128)(2,1)S(1)}, u32[]{:S(2)}, u32[]{:S(2)}) collective-permute-start(bf16[512,128]{1,0:T(8,128)(2,1)S(1)} %get-tuple-element.69.piece), channel_id=1, source_target_pairs={{0,2},{1,3},{2,0},{3,1},{4,6},{5,7},{6,4},{7,5},{8,10},{9,11},{10,... | collective-permute-start | bytes 393224 | tf_op jit(solution)/shard_map/ppermute | solution.py:237
  72.4 6.7 %collective-permute-start.13 = (bf16[512,128]{1,0:T(8,128)(2,1)S(1)}, bf16[512,128]{1,0:T(8,128)(2,1)S(1)}, u32[]{:S(2)}, u32[]{:S(2)}) collective-permute-start(bf16[512,128]{1,0:T(8,128)(2,1)S(1)} %get-tuple-element.69.piece), channel_id=1, source_target_pairs={{0,6},{1,7},{2,4},{3,5},{4,2},{5,3},{6,0},{7,1},{8,14},{9,15},{10,... | collective-permute-start | bytes 393224 | tf_op jit(solution)/shard_map/ppermute | solution.py:237
  74.1 7.0 %collective-permute-start.11 = (bf16[512,128]{1,0:T(8,128)(2,1)S(1)}, bf16[512,128]{1,0:T(8,128)(2,1)S(1)}, u32[]{:S(2)}, u32[]{:S(2)}) collective-permute-start(bf16[512,128]{1,0:T(8,128)(2,1)S(1)} %get-tuple-element.69.piece), channel_id=1, source_target_pairs={{0,4},{1,5},{2,6},{3,7},{4,0},{5,1},{6,2},{7,3},{8,12},{9,13},{10,... | collective-permute-start | bytes 393224 | tf_op jit(solution)/shard_map/ppermute | solution.py:237
  78.1 4.3 %collective-permute-start.16 = (bf16[512,128]{1,0:T(8,128)(2,1)S(1)}, bf16[512,128]{1,0:T(8,128)(2,1)S(1)}, u32[]{:S(2)}, u32[]{:S(2)}) collective-permute-start(bf16[512,128]{1,0:T(8,128)(2,1)S(1)} %collective-permute-done.15.near), channel_id=1, source_target_pairs={{0,1},{1,0},{2,3},{3,2},{4,5},{5,4},{6,7},{7,6},{8,9},{9,8},{10,11... | collective-permute-start | bytes 393224 | tf_op jit(solution)/shard_map/ppermute | solution.py:246
  110.6 5.8 %collective-permute-start.22 = (bf16[512,128]{1,0:T(8,128)(2,1)S(1)}, bf16[512,128]{1,0:T(8,128)(2,1)S(1)}, u32[]{:S(2)}, u32[]{:S(2)}) collective-permute-start(bf16[512,128]{1,0:T(8,128)(2,1)S(1)} %get-tuple-element.78.piece), channel_id=1, source_target_pairs={{0,2},{1,3},{2,0},{3,1},{4,6},{5,7},{6,4},{7,5},{8,10},{9,11},{10,... | collective-permute-start | bytes 393224 | tf_op jit(solution)/shard_map/ppermute | solution.py:237
  111.1 6.0 %collective-permute-start.20 = (bf16[512,128]{1,0:T(8,128)(2,1)S(1)}, bf16[512,128]{1,0:T(8,128)(2,1)S(1)}, u32[]{:S(2)}, u32[]{:S(2)}) collective-permute-start(bf16[512,128]{1,0:T(8,128)(2,1)S(1)} %get-tuple-element.78.piece), channel_id=1, source_target_pairs={{0,6},{1,7},{2,4},{3,5},{4,2},{5,3},{6,0},{7,1},{8,14},{9,15},{10,... | collective-permute-start | bytes 393224 | tf_op jit(solution)/shard_map/ppermute | solution.py:237
  112.6 7.5 %collective-permute-start.18 = (bf16[512,128]{1,0:T(8,128)(2,1)S(1)}, bf16[512,128]{1,0:T(8,128)(2,1)S(1)}, u32[]{:S(2)}, u32[]{:S(2)}) collective-permute-start(bf16[512,128]{1,0:T(8,128)(2,1)S(1)} %get-tuple-element.78.piece), channel_id=1, source_target_pairs={{0,4},{1,5},{2,6},{3,7},{4,0},{5,1},{6,2},{7,3},{8,12},{9,13},{10,... | collective-permute-start | bytes 393224 | tf_op jit(solution)/shard_map/ppermute | solution.py:237
  116.4 4.6 %collective-permute-start.23 = (bf16[512,128]{1,0:T(8,128)(2,1)S(1)}, bf16[512,128]{1,0:T(8,128)(2,1)S(1)}, u32[]{:S(2)}, u32[]{:S(2)}) collective-permute-start(bf16[512,128]{1,0:T(8,128)(2,1)S(1)} %collective-permute-done.22.refs_0_), channel_id=1, source_target_pairs={{0,1},{1,0},{2,3},{3,2},{4,5},{5,4},{6,7},{7,6},{8,9},{9,8},{10,11... | collective-permute-start | bytes 393224 | tf_op jit(solution)/shard_map/ppermute | solution.py:246
  117.1 5.4 %collective-permute-start.21 = (bf16[512,128]{1,0:T(8,128)(2,1)S(1)}, bf16[512,128]{1,0:T(8,128)(2,1)S(1)}, u32[]{:S(2)}, u32[]{:S(2)}) collective-permute-start(bf16[512,128]{1,0:T(8,128)(2,1)S(1)} %collective-permute-done.20.refs_2_), channel_id=1, source_target_pairs={{0,1},{1,0},{2,3},{3,2},{4,5},{5,4},{6,7},{7,6},{8,9},{9,8},{10,11... | collective-permute-start | bytes 393224 | tf_op jit(solution)/shard_map/ppermute | solution.py:246
  124.0 5.8 %collective-permute-start.28 = (bf16[512,128]{1,0:T(8,128)(2,1)S(1)}, bf16[512,128]{1,0:T(8,128)(2,1)S(1)}, u32[]{:S(2)}, u32[]{:S(2)}) collective-permute-start(bf16[512,128]{1,0:T(8,128)(2,1)S(1)} %get-tuple-element.85.piece), channel_id=1, source_target_pairs={{0,2},{1,3},{2,0},{3,1},{4,6},{5,7},{6,4},{7,5},{8,10},{9,11},{10,... | collective-permute-start | bytes 393224 | tf_op jit(solution)/shard_map/ppermute | solution.py:237
  124.1 6.4 %collective-permute-start.26 = (bf16[512,128]{1,0:T(8,128)(2,1)S(1)}, bf16[512,128]{1,0:T(8,128)(2,1)S(1)}, u32[]{:S(2)}, u32[]{:S(2)}) collective-permute-start(bf16[512,128]{1,0:T(8,128)(2,1)S(1)} %get-tuple-element.85.piece), channel_id=1, source_target_pairs={{0,6},{1,7},{2,4},{3,5},{4,2},{5,3},{6,0},{7,1},{8,14},{9,15},{10,... | collective-permute-start | bytes 393224 | tf_op jit(solution)/shard_map/ppermute | solution.py:237
  125.7 7.0 %collective-permute-start.24 = (bf16[512,128]{1,0:T(8,128)(2,1)S(1)}, bf16[512,128]{1,0:T(8,128)(2,1)S(1)}, u32[]{:S(2)}, u32[]{:S(2)}) collective-permute-start(bf16[512,128]{1,0:T(8,128)(2,1)S(1)} %get-tuple-element.85.piece), channel_id=1, source_target_pairs={{0,4},{1,5},{2,6},{3,7},{4,0},{5,1},{6,2},{7,3},{8,12},{9,13},{10,... | collective-permute-start | bytes 393224 | tf_op jit(solution)/shard_map/ppermute | solution.py:237
  129.8 4.3 %collective-permute-start.29 = (bf16[512,128]{1,0:T(8,128)(2,1)S(1)}, bf16[512,128]{1,0:T(8,128)(2,1)S(1)}, u32[]{:S(2)}, u32[]{:S(2)}) collective-permute-start(bf16[512,128]{1,0:T(8,128)(2,1)S(1)} %collective-permute-done.28.near), channel_id=1, source_target_pairs={{0,1},{1,0},{2,3},{3,2},{4,5},{5,4},{6,7},{7,6},{8,9},{9,8},{10,11... | collective-permute-start | bytes 393224 | tf_op jit(solution)/shard_map/ppermute | solution.py:246
  130.4 4.4 %collective-permute-start.27 = (bf16[512,128]{1,0:T(8,128)(2,1)S(1)}, bf16[512,128]{1,0:T(8,128)(2,1)S(1)}, u32[]{:S(2)}, u32[]{:S(2)}) collective-permute-start(bf16[512,128]{1,0:T(8,128)(2,1)S(1)} %collective-permute-done.26.refs_2_), channel_id=1, source_target_pairs={{0,1},{1,0},{2,3},{3,2},{4,5},{5,4},{6,7},{7,6},{8,9},{9,8},{10,11... | collective-permute-start | bytes 393224 | tf_op jit(solution)/shard_map/ppermute | solution.py:246
  162.3 5.8 %collective-permute-start.35 = (bf16[512,128]{1,0:T(8,128)(2,1)S(1)}, bf16[512,128]{1,0:T(8,128)(2,1)S(1)}, u32[]{:S(2)}, u32[]{:S(2)}) collective-permute-start(bf16[512,128]{1,0:T(8,128)(2,1)S(1)} %get-tuple-element.94.piece), channel_id=1, source_target_pairs={{0,2},{1,3},{2,0},{3,1},{4,6},{5,7},{6,4},{7,5},{8,10},{9,11},{10,... | collective-permute-start | bytes 393224 | tf_op jit(solution)/shard_map/ppermute | solution.py:237
  162.8 6.0 %collective-permute-start.33 = (bf16[512,128]{1,0:T(8,128)(2,1)S(1)}, bf16[512,128]{1,0:T(8,128)(2,1)S(1)}, u32[]{:S(2)}, u32[]{:S(2)}) collective-permute-start(bf16[512,128]{1,0:T(8,128)(2,1)S(1)} %get-tuple-element.94.piece), channel_id=1, source_target_pairs={{0,6},{1,7},{2,4},{3,5},{4,2},{5,3},{6,0},{7,1},{8,14},{9,15},{10,... | collective-permute-start | bytes 393224 | tf_op jit(solution)/shard_map/ppermute | solution.py:237
  164.2 8.5 %collective-permute-start.31 = (bf16[512,128]{1,0:T(8,128)(2,1)S(1)}, bf16[512,128]{1,0:T(8,128)(2,1)S(1)}, u32[]{:S(2)}, u32[]{:S(2)}) collective-permute-start(bf16[512,128]{1,0:T(8,128)(2,1)S(1)} %get-tuple-element.94.piece), channel_id=1, source_target_pairs={{0,4},{1,5},{2,6},{3,7},{4,0},{5,1},{6,2},{7,3},{8,12},{9,13},{10,... | collective-permute-start | bytes 393224 | tf_op jit(solution)/shard_map/ppermute | solution.py:237
  168.1 4.6 %collective-permute-start.36 = (bf16[512,128]{1,0:T(8,128)(2,1)S(1)}, bf16[512,128]{1,0:T(8,128)(2,1)S(1)}, u32[]{:S(2)}, u32[]{:S(2)}) collective-permute-start(bf16[512,128]{1,0:T(8,128)(2,1)S(1)} %collective-permute-done.35.refs_0_), channel_id=1, source_target_pairs={{0,1},{1,0},{2,3},{3,2},{4,5},{5,4},{6,7},{7,6},{8,9},{9,8},{10,11... | collective-permute-start | bytes 393224 | tf_op jit(solution)/shard_map/ppermute | solution.py:246
  168.8 5.4 %collective-permute-start.34 = (bf16[512,128]{1,0:T(8,128)(2,1)S(1)}, bf16[512,128]{1,0:T(8,128)(2,1)S(1)}, u32[]{:S(2)}, u32[]{:S(2)}) collective-permute-start(bf16[512,128]{1,0:T(8,128)(2,1)S(1)} %collective-permute-done.33.refs_2_), channel_id=1, source_target_pairs={{0,1},{1,0},{2,3},{3,2},{4,5},{5,4},{6,7},{7,6},{8,9},{9,8},{10,11... | collective-permute-start | bytes 393224 | tf_op jit(solution)/shard_map/ppermute | solution.py:246
  175.6 6.3 %collective-permute-start.41 = (bf16[512,128]{1,0:T(8,128)(2,1)S(1)}, bf16[512,128]{1,0:T(8,128)(2,1)S(1)}, u32[]{:S(2)}, u32[]{:S(2)}) collective-permute-start(bf16[512,128]{1,0:T(8,128)(2,1)S(1)} %get-tuple-element.102.refs_3_), channel_id=1, source_target_pairs={{0,2},{1,3},{2,0},{3,1},{4,6},{5,7},{6,4},{7,5},{8,10},{9,11},{10,... | collective-permute-start | bytes 393224 | tf_op jit(solution)/shard_map/ppermute | solution.py:237
  175.7 6.8 %collective-permute-start.39 = (bf16[512,128]{1,0:T(8,128)(2,1)S(1)}, bf16[512,128]{1,0:T(8,128)(2,1)S(1)}, u32[]{:S(2)}, u32[]{:S(2)}) collective-permute-start(bf16[512,128]{1,0:T(8,128)(2,1)S(1)} %get-tuple-element.102.refs_3_), channel_id=1, source_target_pairs={{0,6},{1,7},{2,4},{3,5},{4,2},{5,3},{6,0},{7,1},{8,14},{9,15},{10,... | collective-permute-start | bytes 393224 | tf_op jit(solution)/shard_map/ppermute | solution.py:237
  177.4 8.4 %collective-permute-start.37 = (bf16[512,128]{1,0:T(8,128)(2,1)S(1)}, bf16[512,128]{1,0:T(8,128)(2,1)S(1)}, u32[]{:S(2)}, u32[]{:S(2)}) collective-permute-start(bf16[512,128]{1,0:T(8,128)(2,1)S(1)} %get-tuple-element.102.refs_3_), channel_id=1, source_target_pairs={{0,4},{1,5},{2,6},{3,7},{4,0},{5,1},{6,2},{7,3},{8,12},{9,13},{10,... | collective-permute-start | bytes 393224 | tf_op jit(solution)/shard_map/ppermute | solution.py:237
  (17 other events, 105.6 us)

commit v3 on v2

--- a/solution.py
+++ b/solution.py
@@ -1,3 +1,5 @@
+import functools
+
 import jax
 import jax.numpy as jnp
 from jax import lax
@@ -187,18 +189,18 @@
         copy.wait()
 
 
-def drive_kernel(*refs):
+def drive_kernel(start, *refs):
     out, leak_out, weight, stimulus, bias, leak, done = refs[-7:]
     fetch(refs[:4], (weight, stimulus, bias, leak), done)
     leak_out[...] = column(leak[...])
     base = column(bias[...])
 
     def one(n, carry):
-        part = lax.dot_general(weight[...], stimulus[n], (((0,), (0,)), ((), ())), preferred_element_type=F32)
+        part = lax.dot_general(weight[...], stimulus[start + n], (((0,), (0,)), ((), ())), preferred_element_type=F32)
         out[n] = part + base
         return carry
 
-    lax.fori_loop(0, 2 * WINDOWS, one, 0)
+    lax.fori_loop(0, out.shape[0], one, 0)
 
 
 def both_kernel(rates, prior, out, rates_here, done):
@@ -284,14 +286,19 @@
     weight_local = local_weight[0]
     weight_long = long_weight[0]
     inputs = [input_weight[0].T, stimulus, unit_bias, leak_rate]
-    drives, leak = call(
-        drive_kernel,
-        inputs,
-        (jax.ShapeDtypeStruct((2 * WINDOWS, ROWS, BLOCK), F32), shape(ROWS, F32)),
-        1000,
-        [*(pltpu.VMEM(x.shape, x.dtype) for x in inputs[:4]), pltpu.SemaphoreType.DMA((4,))],
-        far=4,
-    )
+
+    def driven(start, count):
+        return call(
+            functools.partial(drive_kernel, start),
+            inputs,
+            (jax.ShapeDtypeStruct((count, ROWS, BLOCK), F32), shape(ROWS, F32)),
+            1000,
+            [*(pltpu.VMEM(x.shape, x.dtype) for x in inputs[:4]), pltpu.SemaphoreType.DMA((4,))],
+            far=4,
+        )
+
+    drives, leak = driven(0, 2)
+    late_drives, _ = driven(2, 2 * WINDOWS - 2)
     flops = ROWS * UNITS * BLOCK
 
     def long_range(outgoing):
@@ -323,7 +330,7 @@
     def window(step, carry):
         later, outgoing, rates = carry
         mine, theirs = long_range(outgoing)
-        drive = [drives[2 * step + n] for n in range(2)]
+        drive = [drives[n] if step == 0 else late_drives[2 * step + n - 2] for n in range(2)]
         partial = call(local_kernel, [table, weight_local, *later, drive[0]], shape(ROWS, F32), 2 * flops)
         current, rates, copy = call(
             first_kernel,

time: 215 us -> 235 us (1.093)
  waiting for transfers between devices: 6.84 us -> 25.6 us
  starting transfers between devices: 55 us -> 48.9 us
  local copies, waits for them, and re-layouts: 1.01 us -> 5.49 us
    ppermute x21, waiting for transfers between devices: 5.06 us -> 24.2 us  [neighbours(): found.append(lax.ppermute(piece, 'unit', [(u, u ^ m) for u in range(8)]))]
    ppermute x18, starting transfers between devices: 21.7 us -> 12.3 us  [exchange(): pieces += [x, lax.ppermute(x, 'unit', PAIRS)]]
    ppermute x21, starting transfers between devices: 24.9 us -> 28.2 us  [neighbours(): found.append(lax.ppermute(piece, 'unit', [(u, u ^ m) for u in range(8)]))]
    unnamed x10 -> x22, local copies, waits for them, and re-layouts: 0.03 us -> 3.27 us
    pallas_call x23 -> x24, Pallas kernels: 32.3 us -> 34.4 us  [call(): pl.pallas_call(kernel, out_shape=outs, in_specs=[HBM if i < far else SMEM...]
  transfers between devices with their start and end apart: 44 -> 44, of which waited for: 11 -> 17; matrix products, arithmetic and copies ran while one was open for 1% -> 2% of each run, Pallas kernels for 8% -> 8%
where the time goes in v3:
time: 235 us; the launch traced here: 234 us
  blocking collectives  117 us (50%)
  starting transfers between devices  48.9 us (21%)
  Pallas kernels  34.4 us (15%)
  waiting for transfers between devices  25.6 us (11%)
  local copies, waits for them, and re-layouts  5.49 us (2%)
    all_to_all x4, blocking collectives, long_range(): lax.all_to_all(outgoing, 'area', split_axis=0, concat_axis=0, tiled=True)  91.8 us
    pallas_call x24, Pallas kernels, call(): pl.pallas_call(kernel, out_shape=outs, in_specs=[HBM if i < far else SMEM...  34.4 us
    ppermute x21, starting transfers between devices, neighbours(): found.append(lax.ppermute(piece, 'unit', [(u, u ^ m) for u in range(8)]))  28.2 us
    all_gather x9, blocking collectives, paired(): lax.all_gather(piece, 'unit', axis=0, tiled=True, axis_index_groups=[[0,...  25.2 us
    ppermute x21, waiting for transfers between devices, neighbours(): found.append(lax.ppermute(piece, 'unit', [(u, u ^ m) for u in range(8)]))  24.2 us
    ppermute x18, starting transfers between devices, exchange(): pieces += [x, lax.ppermute(x, 'unit', PAIRS)]  12.3 us
    ppermute x4, starting transfers between devices, long_range(): other = lax.ppermute(arrived, 'unit', PAIRS)  7.98 us
  transfers between devices with their start and end apart: 44, of which 17 were waited for; matrix products, arithmetic and copies ran while one was open for 2% of the time, Pallas kernels for 8%

profile of v3, /device:TPU:1, one launch (start us, length us, event | category | flops | bytes accessed | tf_op | source)
XLA Modules:
  0.0 234.5 jit_solution(3541669572901079779)
XLA Ops:
  2.4 3.8 %collective-permute-start.1 = (bf16[1024,128]{1,0:T(8,128)(2,1)}, bf16[1024,128]{1,0:T(8,128)(2,1)S(1)}, u32[]{:S(2)}, u32[]{:S(2)}) collective-permute-start(bf16[1024,128]{1,0:T(8,128)(2,1)} %shard_map.122), channel_id=1, source_target_pairs={{0,4},{1,5},{2,6},{3,7},{4,0},{5,1},{6,2},{7,3},{8,12},{9,13},{10,... | collective-permute-start | bytes 786440 | tf_op jit(solution)/shard_map/ppermute | solution.py:239
  9.6 2.3 shard_map.123
  12.0 4.9 %all_gather.27.own = bf16[2048,128]{1,0:T(8,128)(2,1)S(1)} all-gather(bf16[1024,128]{1,0:T(8,128)(2,1)} %shard_map.122), channel_id=1, replica_groups={{0,1},{2,3},{4,5},{6,7},{8,9},{10,11},{12,13},{14,15},{16,17},{18,19},{..., dimensions={0}, use_global_device_ids=true | all-gather | bytes 786432 | tf_op jit(solution)/shard_map/all_gather | solution.py:230
  18.2 3.3 %all_gather.28.near = bf16[2048,128]{1,0:T(8,128)(2,1)S(1)} all-gather(bf16[1024,128]{1,0:T(8,128)(2,1)S(1)} %collective-permute-done), channel_id=1, replica_groups={{0,1},{2,3},{4,5},{6,7},{8,9},{10,11},{12,13},{14,15},{16,17},{18,19},{..., dimensions={0}, use_global_device_ids=true | all-gather | bytes 786432 | tf_op jit(solution)/shard_map/all_gather | solution.py:230
  21.5 2.2 all_gather.29.second
  24.6 28.1 %all_to_all.20.mine = bf16[32,64,128]{2,1,0:T(8,128)(2,1)S(1)} all-to-all(bf16[32,64,128]{2,1,0:T(8,128)(2,1)S(1)} %get-tuple-element.58), channel_id=1, replica_groups=mesh['area'=32,'unit'=8] {'area'}, dimensions={0} | all-to-all | bytes 1048576 | tf_op jit(solution)/shard_map/all_to_all | solution.py:305
  52.7 2.1 collective-permute-start.4
  60.2 2.2 collective-permute-start.7
  62.4 2.5 %all_gather.30.pair = bf16[1024,128]{1,0:T(8,128)(2,1)S(1)} all-gather(bf16[512,128]{1,0:T(8,128)(2,1)S(1)} %get-tuple-element.63.piece), channel_id=1, replica_groups={{0,1},{2,3},{4,5},{6,7},{8,9},{10,11},{12,13},{14,15},{16,17},{18,19},{..., dimensions={0}, use_global_device_ids=true | all-gather | bytes 393216 | tf_op jit(solution)/shard_map/all_gather | solution.py:230
  73.0 3.3 %collective-permute-start.11 = (bf16[512,128]{1,0:T(8,128)(2,1)S(1)}, bf16[512,128]{1,0:T(8,128)(2,1)S(1)}, u32[]{:S(2)}, u32[]{:S(2)}) collective-permute-start(bf16[512,128]{1,0:T(8,128)(2,1)S(1)} %get-tuple-element.70.piece), channel_id=1, source_target_pairs={{0,4},{1,5},{2,6},{3,7},{4,0},{5,1},{6,2},{7,3},{8,12},{9,13},{10,... | collective-permute-start | bytes 393224 | tf_op jit(solution)/shard_map/ppermute | solution.py:239
  76.9 2.5 %all_gather.31.pair = bf16[1024,128]{1,0:T(8,128)(2,1)S(1)} all-gather(bf16[512,128]{1,0:T(8,128)(2,1)S(1)} %get-tuple-element.70.piece), channel_id=1, replica_groups={{0,1},{2,3},{4,5},{6,7},{8,9},{10,11},{12,13},{14,15},{16,17},{18,19},{..., dimensions={0}, use_global_device_ids=true | all-gather | bytes 393216 | tf_op jit(solution)/shard_map/all_gather | solution.py:230
  79.7 3.0 %collective-permute-done.11.refs_0_ = bf16[512,128]{1,0:T(8,128)(2,1)S(1)} collective-permute-done((bf16[512,128]{1,0:T(8,128)(2,1)S(1)}, bf16[512,128]{1,0:T(8,128)(2,1)S(1)}, u32[]{:S(2)}, u32[]{:S(2)}) %collective-permute-start.11) | collective-permute-done | bytes 131104 | tf_op jit(solution)/shard_map/ppermute | solution.py:239
  87.7 21.2 %all_to_all.21.mine = bf16[32,64,128]{2,1,0:T(8,128)(2,1)S(1)} all-to-all(bf16[32,64,128]{2,1,0:T(8,128)(2,1)S(1)} %get-tuple-element.75), channel_id=1, replica_groups=mesh['area'=32,'unit'=8] {'area'}, dimensions={0} | all-to-all | bytes 1048576 | tf_op jit(solution)/shard_map/all_to_all | solution.py:305
  108.9 1.9 collective-permute-start.17
  110.9 2.9 %shard_map.131 = (f32[4,512,128]{2,1,0:T(8,128)}, f32[512,128]{1,0:T(8,128)}) custom-call(bf16[16,512]{1,0:T(8,128)(2,1)} %bitcast.40, bf16[6,16,128]{2,1,0:T(8,128)(2,1)} %refs_1_.3, f32[1,512]{1,0:T(1,128)} %refs_2_.3, f32[1,512]{1,0:T(1,128)} %refs_3_.3), custom_call_target="tpu_custom_call" | custom-call | flops 1000 | bytes 45056 | tf_op jit(solution)/shard_map/pallas_call | solution.py:213
  115.1 2.2 copy-done.1
  120.3 2.0 shard_map.133
  124.2 2.1 collective-permute-start.20
  126.2 2.5 %all_gather.32.pair = bf16[1024,128]{1,0:T(8,128)(2,1)S(1)} all-gather(bf16[512,128]{1,0:T(8,128)(2,1)S(1)} %get-tuple-element.80.piece), channel_id=1, replica_groups={{0,1},{2,3},{4,5},{6,7},{8,9},{10,11},{12,13},{14,15},{16,17},{18,19},{..., dimensions={0}, use_global_device_ids=true | all-gather | bytes 393216 | tf_op jit(solution)/shard_map/all_gather | solution.py:230
  137.0 3.2 %collective-permute-start.24 = (bf16[512,128]{1,0:T(8,128)(2,1)S(1)}, bf16[512,128]{1,0:T(8,128)(2,1)S(1)}, u32[]{:S(2)}, u32[]{:S(2)}) collective-permute-start(bf16[512,128]{1,0:T(8,128)(2,1)S(1)} %get-tuple-element.87.piece), channel_id=1, source_target_pairs={{0,4},{1,5},{2,6},{3,7},{4,0},{5,1},{6,2},{7,3},{8,12},{9,13},{10,... | collective-permute-start | bytes 393224 | tf_op jit(solution)/shard_map/ppermute | solution.py:239
  140.8 2.5 %all_gather.33.pair = bf16[1024,128]{1,0:T(8,128)(2,1)S(1)} all-gather(bf16[512,128]{1,0:T(8,128)(2,1)S(1)} %get-tuple-element.87.piece), channel_id=1, replica_groups={{0,1},{2,3},{4,5},{6,7},{8,9},{10,11},{12,13},{14,15},{16,17},{18,19},{..., dimensions={0}, use_global_device_ids=true | all-gather | bytes 393216 | tf_op jit(solution)/shard_map/all_gather | solution.py:230
  143.7 3.0 %collective-permute-done.24.refs_0_ = bf16[512,128]{1,0:T(8,128)(2,1)S(1)} collective-permute-done((bf16[512,128]{1,0:T(8,128)(2,1)S(1)}, bf16[512,128]{1,0:T(8,128)(2,1)S(1)}, u32[]{:S(2)}, u32[]{:S(2)}) %collective-permute-start.24) | collective-permute-done | bytes 131104 | tf_op jit(solution)/shard_map/ppermute | solution.py:239
  151.6 21.3 %all_to_all.22.mine = bf16[32,64,128]{2,1,0:T(8,128)(2,1)S(1)} all-to-all(bf16[32,64,128]{2,1,0:T(8,128)(2,1)S(1)} %get-tuple-element.92), channel_id=1, replica_groups=mesh['area'=32,'unit'=8] {'area'}, dimensions={0} | all-to-all | bytes 1048576 | tf_op jit(solution)/shard_map/all_to_all | solution.py:305
  172.9 1.9 collective-permute-start.30
  180.2 2.1 collective-permute-start.33
  182.2 2.5 %all_gather.34.pair = bf16[1024,128]{1,0:T(8,128)(2,1)S(1)} all-gather(bf16[512,128]{1,0:T(8,128)(2,1)S(1)} %get-tuple-element.96.piece), channel_id=1, replica_groups={{0,1},{2,3},{4,5},{6,7},{8,9},{10,11},{12,13},{14,15},{16,17},{18,19},{..., dimensions={0}, use_global_device_ids=true | all-gather | bytes 393216 | tf_op jit(solution)/shard_map/all_gather | solution.py:230
  193.0 3.2 %collective-permute-start.37 = (bf16[512,128]{1,0:T(8,128)(2,1)S(1)}, bf16[512,128]{1,0:T(8,128)(2,1)S(1)}, u32[]{:S(2)}, u32[]{:S(2)}) collective-permute-start(bf16[512,128]{1,0:T(8,128)(2,1)S(1)} %get-tuple-element.104.refs_3_), channel_id=1, source_target_pairs={{0,4},{1,5},{2,6},{3,7},{4,0},{5,1},{6,2},{7,3},{8,12},{9,13},{10,... | collective-permute-start | bytes 393224 | tf_op jit(solution)/shard_map/ppermute | solution.py:239
  196.8 2.5 %all_gather.35.refs_4_ = bf16[1024,128]{1,0:T(8,128)(2,1)S(1)} all-gather(bf16[512,128]{1,0:T(8,128)(2,1)S(1)} %get-tuple-element.104.refs_3_), channel_id=1, replica_groups={{0,1},{2,3},{4,5},{6,7},{8,9},{10,11},{12,13},{14,15},{16,17},{18,19},{..., dimensions={0}, use_global_device_ids=true | all-gather | bytes 393216 | tf_op jit(solution)/shard_map/all_gather | solution.py:230
  199.7 3.0 %collective-permute-done.37.refs_3_ = bf16[512,128]{1,0:T(8,128)(2,1)S(1)} collective-permute-done((bf16[512,128]{1,0:T(8,128)(2,1)S(1)}, bf16[512,128]{1,0:T(8,128)(2,1)S(1)}, u32[]{:S(2)}, u32[]{:S(2)}) %collective-permute-start.37) | collective-permute-done | bytes 131104 | tf_op jit(solution)/shard_map/ppermute | solution.py:239
  207.6 21.3 %all_to_all.23.mine = bf16[32,64,128]{2,1,0:T(8,128)(2,1)S(1)} all-to-all(bf16[32,64,128]{2,1,0:T(8,128)(2,1)S(1)} %shard_map.144), channel_id=1, replica_groups=mesh['area'=32,'unit'=8] {'area'}, dimensions={0} | all-to-all | bytes 1048576 | tf_op jit(solution)/shard_map/all_to_all | solution.py:305
  228.8 1.9 collective-permute-start.43
  232.3 2.2 shard_map.145
  (128 shorter events, 68.0 us)
Async XLA Ops:
  2.4 14.6 %collective-permute-start.1 = (bf16[1024,128]{1,0:T(8,128)(2,1)}, bf16[1024,128]{1,0:T(8,128)(2,1)S(1)}, u32[]{:S(2)}, u32[]{:S(2)}) collective-permute-start(bf16[1024,128]{1,0:T(8,128)(2,1)} %shard_map.122), channel_id=1, source_target_pairs={{0,4},{1,5},{2,6},{3,7},{4,0},{5,1},{6,2},{7,3},{8,12},{9,13},{10,... | collective-permute-start | bytes 786440 | tf_op jit(solution)/shard_map/ppermute | solution.py:239
  6.2 12.0 %collective-permute-start = (bf16[1024,128]{1,0:T(8,128)(2,1)}, bf16[1024,128]{1,0:T(8,128)(2,1)S(1)}, u32[]{:S(2)}, u32[]{:S(2)}) collective-permute-start(bf16[1024,128]{1,0:T(8,128)(2,1)} %shard_map.122), channel_id=1, source_target_pairs={{0,2},{1,3},{2,0},{3,1},{4,6},{5,7},{6,4},{7,5},{8,10},{9,11},{10,... | collective-permute-start | bytes 786440 | tf_op jit(solution)/shard_map/ppermute | solution.py:239
  6.6 14.9 %collective-permute-start.3 = (bf16[1024,128]{1,0:T(8,128)(2,1)}, bf16[1024,128]{1,0:T(8,128)(2,1)S(1)}, u32[]{:S(2)}, u32[]{:S(2)}) collective-permute-start(bf16[1024,128]{1,0:T(8,128)(2,1)} %shard_map.122), channel_id=1, source_target_pairs={{0,6},{1,7},{2,4},{3,5},{4,2},{5,3},{6,0},{7,1},{8,14},{9,15},{10,... | collective-permute-start | bytes 786440 | tf_op jit(solution)/shard_map/ppermute | solution.py:239
  17.0 6.7 %collective-permute-start.2 = (bf16[1024,128]{1,0:T(8,128)(2,1)S(1)}, bf16[1024,128]{1,0:T(8,128)(2,1)S(1)}, u32[]{:S(2)}, u32[]{:S(2)}) collective-permute-start(bf16[1024,128]{1,0:T(8,128)(2,1)S(1)} %collective-permute-done.1.far), channel_id=1, source_target_pairs={{0,1},{1,0},{2,3},{3,2},{4,5},{5,4},{6,7},{7,6},{8,9},{9,8},{10,11... | collective-permute-start | bytes 786440 | tf_op jit(solution)/shard_map/ppermute | solution.py:325
  58.4 6.4 %collective-permute-start.9 = (bf16[512,128]{1,0:T(8,128)(2,1)S(1)}, bf16[512,128]{1,0:T(8,128)(2,1)S(1)}, u32[]{:S(2)}, u32[]{:S(2)}) collective-permute-start(bf16[512,128]{1,0:T(8,128)(2,1)S(1)} %get-tuple-element.63.piece), channel_id=1, source_target_pairs={{0,2},{1,3},{2,0},{3,1},{4,6},{5,7},{6,4},{7,5},{8,10},{9,11},{10,... | collective-permute-start | bytes 393224 | tf_op jit(solution)/shard_map/ppermute | solution.py:239
  59.6 7.0 %collective-permute-start.5 = (bf16[512,128]{1,0:T(8,128)(2,1)S(1)}, bf16[512,128]{1,0:T(8,128)(2,1)S(1)}, u32[]{:S(2)}, u32[]{:S(2)}) collective-permute-start(bf16[512,128]{1,0:T(8,128)(2,1)S(1)} %get-tuple-element.63.piece), channel_id=1, source_target_pairs={{0,4},{1,5},{2,6},{3,7},{4,0},{5,1},{6,2},{7,3},{8,12},{9,13},{10,... | collective-permute-start | bytes 393224 | tf_op jit(solution)/shard_map/ppermute | solution.py:239
  60.2 9.2 %collective-permute-start.7 = (bf16[512,128]{1,0:T(8,128)(2,1)S(1)}, bf16[512,128]{1,0:T(8,128)(2,1)S(1)}, u32[]{:S(2)}, u32[]{:S(2)}) collective-permute-start(bf16[512,128]{1,0:T(8,128)(2,1)S(1)} %get-tuple-element.63.piece), channel_id=1, source_target_pairs={{0,6},{1,7},{2,4},{3,5},{4,2},{5,3},{6,0},{7,1},{8,14},{9,15},{10,... | collective-permute-start | bytes 393224 | tf_op jit(solution)/shard_map/ppermute | solution.py:239
  64.8 5.2 %collective-permute-start.10 = (bf16[512,128]{1,0:T(8,128)(2,1)S(1)}, bf16[512,128]{1,0:T(8,128)(2,1)S(1)}, u32[]{:S(2)}, u32[]{:S(2)}) collective-permute-start(bf16[512,128]{1,0:T(8,128)(2,1)S(1)} %collective-permute-done.9.refs_0_), channel_id=1, source_target_pairs={{0,1},{1,0},{2,3},{3,2},{4,5},{5,4},{6,7},{7,6},{8,9},{9,8},{10,11... | collective-permute-start | bytes 393224 | tf_op jit(solution)/shard_map/ppermute | solution.py:248
  66.6 4.8 %collective-permute-start.6 = (bf16[512,128]{1,0:T(8,128)(2,1)S(1)}, bf16[512,128]{1,0:T(8,128)(2,1)S(1)}, u32[]{:S(2)}, u32[]{:S(2)}) collective-permute-start(bf16[512,128]{1,0:T(8,128)(2,1)S(1)} %collective-permute-done.5.refs_0_), channel_id=1, source_target_pairs={{0,1},{1,0},{2,3},{3,2},{4,5},{5,4},{6,7},{7,6},{8,9},{9,8},{10,11... | collective-permute-start | bytes 393224 | tf_op jit(solution)/shard_map/ppermute | solution.py:248
  72.9 6.4 %collective-permute-start.15 = (bf16[512,128]{1,0:T(8,128)(2,1)S(1)}, bf16[512,128]{1,0:T(8,128)(2,1)S(1)}, u32[]{:S(2)}, u32[]{:S(2)}) collective-permute-start(bf16[512,128]{1,0:T(8,128)(2,1)S(1)} %get-tuple-element.70.piece), channel_id=1, source_target_pairs={{0,2},{1,3},{2,0},{3,1},{4,6},{5,7},{6,4},{7,5},{8,10},{9,11},{10,... | collective-permute-start | bytes 393224 | tf_op jit(solution)/shard_map/ppermute | solution.py:239
  73.0 9.7 %collective-permute-start.11 = (bf16[512,128]{1,0:T(8,128)(2,1)S(1)}, bf16[512,128]{1,0:T(8,128)(2,1)S(1)}, u32[]{:S(2)}, u32[]{:S(2)}) collective-permute-start(bf16[512,128]{1,0:T(8,128)(2,1)S(1)} %get-tuple-element.70.piece), channel_id=1, source_target_pairs={{0,4},{1,5},{2,6},{3,7},{4,0},{5,1},{6,2},{7,3},{8,12},{9,13},{10,... | collective-permute-start | bytes 393224 | tf_op jit(solution)/shard_map/ppermute | solution.py:239
  76.3 9.0 %collective-permute-start.13 = (bf16[512,128]{1,0:T(8,128)(2,1)S(1)}, bf16[512,128]{1,0:T(8,128)(2,1)S(1)}, u32[]{:S(2)}, u32[]{:S(2)}) collective-permute-start(bf16[512,128]{1,0:T(8,128)(2,1)S(1)} %get-tuple-element.70.piece), channel_id=1, source_target_pairs={{0,6},{1,7},{2,4},{3,5},{4,2},{5,3},{6,0},{7,1},{8,14},{9,15},{10,... | collective-permute-start | bytes 393224 | tf_op jit(solution)/shard_map/ppermute | solution.py:239
  79.4 6.7 %collective-permute-start.16 = (bf16[512,128]{1,0:T(8,128)(2,1)S(1)}, bf16[512,128]{1,0:T(8,128)(2,1)S(1)}, u32[]{:S(2)}, u32[]{:S(2)}) collective-permute-start(bf16[512,128]{1,0:T(8,128)(2,1)S(1)} %collective-permute-done.15.near), channel_id=1, source_target_pairs={{0,1},{1,0},{2,3},{3,2},{4,5},{5,4},{6,7},{7,6},{8,9},{9,8},{10,11... | collective-permute-start | bytes 393224 | tf_op jit(solution)/shard_map/ppermute | solution.py:248
  108.9 11.4 %collective-permute-start.17 = (bf16[32,64,128]{2,1,0:T(8,128)(2,1)S(1)}, bf16[32,64,128]{2,1,0:T(8,128)(2,1)}, u32[]{:S(2)}, u32[]{:S(2)}) collective-permute-start(bf16[32,64,128]{2,1,0:T(8,128)(2,1)S(1)} %all_to_all.21.mine), channel_id=1, source_target_pairs={{0,1},{1,0},{2,3},{3,2},{4,5},{5,4},{6,7},{7,6},{8,9},{9,8},{10,11... | collective-permute-start | bytes 1572872 | tf_op jit(solution)/shard_map/ppermute | solution.py:306
  122.3 6.4 %collective-permute-start.22 = (bf16[512,128]{1,0:T(8,128)(2,1)S(1)}, bf16[512,128]{1,0:T(8,128)(2,1)S(1)}, u32[]{:S(2)}, u32[]{:S(2)}) collective-permute-start(bf16[512,128]{1,0:T(8,128)(2,1)S(1)} %get-tuple-element.80.piece), channel_id=1, source_target_pairs={{0,2},{1,3},{2,0},{3,1},{4,6},{5,7},{6,4},{7,5},{8,10},{9,11},{10,... | collective-permute-start | bytes 393224 | tf_op jit(solution)/shard_map/ppermute | solution.py:239
  122.4 8.2 %collective-permute-start.18 = (bf16[512,128]{1,0:T(8,128)(2,1)S(1)}, bf16[512,128]{1,0:T(8,128)(2,1)S(1)}, u32[]{:S(2)}, u32[]{:S(2)}) collective-permute-start(bf16[512,128]{1,0:T(8,128)(2,1)S(1)} %get-tuple-element.80.piece), channel_id=1, source_target_pairs={{0,4},{1,5},{2,6},{3,7},{4,0},{5,1},{6,2},{7,3},{8,12},{9,13},{10,... | collective-permute-start | bytes 393224 | tf_op jit(solution)/shard_map/ppermute | solution.py:239
  124.2 9.0 %collective-permute-start.20 = (bf16[512,128]{1,0:T(8,128)(2,1)S(1)}, bf16[512,128]{1,0:T(8,128)(2,1)S(1)}, u32[]{:S(2)}, u32[]{:S(2)}) collective-permute-start(bf16[512,128]{1,0:T(8,128)(2,1)S(1)} %get-tuple-element.80.piece), channel_id=1, source_target_pairs={{0,6},{1,7},{2,4},{3,5},{4,2},{5,3},{6,0},{7,1},{8,14},{9,15},{10,... | collective-permute-start | bytes 393224 | tf_op jit(solution)/shard_map/ppermute | solution.py:239
  128.7 5.2 %collective-permute-start.23 = (bf16[512,128]{1,0:T(8,128)(2,1)S(1)}, bf16[512,128]{1,0:T(8,128)(2,1)S(1)}, u32[]{:S(2)}, u32[]{:S(2)}) collective-permute-start(bf16[512,128]{1,0:T(8,128)(2,1)S(1)} %collective-permute-done.22.refs_0_), channel_id=1, source_target_pairs={{0,1},{1,0},{2,3},{3,2},{4,5},{5,4},{6,7},{7,6},{8,9},{9,8},{10,11... | collective-permute-start | bytes 393224 | tf_op jit(solution)/shard_map/ppermute | solution.py:248
  130.6 4.8 %collective-permute-start.19 = (bf16[512,128]{1,0:T(8,128)(2,1)S(1)}, bf16[512,128]{1,0:T(8,128)(2,1)S(1)}, u32[]{:S(2)}, u32[]{:S(2)}) collective-permute-start(bf16[512,128]{1,0:T(8,128)(2,1)S(1)} %collective-permute-done.18.refs_0_), channel_id=1, source_target_pairs={{0,1},{1,0},{2,3},{3,2},{4,5},{5,4},{6,7},{7,6},{8,9},{9,8},{10,11... | collective-permute-start | bytes 393224 | tf_op jit(solution)/shard_map/ppermute | solution.py:248
  136.9 6.4 %collective-permute-start.28 = (bf16[512,128]{1,0:T(8,128)(2,1)S(1)}, bf16[512,128]{1,0:T(8,128)(2,1)S(1)}, u32[]{:S(2)}, u32[]{:S(2)}) collective-permute-start(bf16[512,128]{1,0:T(8,128)(2,1)S(1)} %get-tuple-element.87.piece), channel_id=1, source_target_pairs={{0,2},{1,3},{2,0},{3,1},{4,6},{5,7},{6,4},{7,5},{8,10},{9,11},{10,... | collective-permute-start | bytes 393224 | tf_op jit(solution)/shard_map/ppermute | solution.py:239
  137.0 9.6 %collective-permute-start.24 = (bf16[512,128]{1,0:T(8,128)(2,1)S(1)}, bf16[512,128]{1,0:T(8,128)(2,1)S(1)}, u32[]{:S(2)}, u32[]{:S(2)}) collective-permute-start(bf16[512,128]{1,0:T(8,128)(2,1)S(1)} %get-tuple-element.87.piece), channel_id=1, source_target_pairs={{0,4},{1,5},{2,6},{3,7},{4,0},{5,1},{6,2},{7,3},{8,12},{9,13},{10,... | collective-permute-start | bytes 393224 | tf_op jit(solution)/shard_map/ppermute | solution.py:239
  140.2 9.0 %collective-permute-start.26 = (bf16[512,128]{1,0:T(8,128)(2,1)S(1)}, bf16[512,128]{1,0:T(8,128)(2,1)S(1)}, u32[]{:S(2)}, u32[]{:S(2)}) collective-permute-start(bf16[512,128]{1,0:T(8,128)(2,1)S(1)} %get-tuple-element.87.piece), channel_id=1, source_target_pairs={{0,6},{1,7},{2,4},{3,5},{4,2},{5,3},{6,0},{7,1},{8,14},{9,15},{10,... | collective-permute-start | bytes 393224 | tf_op jit(solution)/shard_map/ppermute | solution.py:239
  143.3 6.7 %collective-permute-start.29 = (bf16[512,128]{1,0:T(8,128)(2,1)S(1)}, bf16[512,128]{1,0:T(8,128)(2,1)S(1)}, u32[]{:S(2)}, u32[]{:S(2)}) collective-permute-start(bf16[512,128]{1,0:T(8,128)(2,1)S(1)} %collective-permute-done.28.near), channel_id=1, source_target_pairs={{0,1},{1,0},{2,3},{3,2},{4,5},{5,4},{6,7},{7,6},{8,9},{9,8},{10,11... | collective-permute-start | bytes 393224 | tf_op jit(solution)/shard_map/ppermute | solution.py:248
  178.3 6.4 %collective-permute-start.35 = (bf16[512,128]{1,0:T(8,128)(2,1)S(1)}, bf16[512,128]{1,0:T(8,128)(2,1)S(1)}, u32[]{:S(2)}, u32[]{:S(2)}) collective-permute-start(bf16[512,128]{1,0:T(8,128)(2,1)S(1)} %get-tuple-element.96.piece), channel_id=1, source_target_pairs={{0,2},{1,3},{2,0},{3,1},{4,6},{5,7},{6,4},{7,5},{8,10},{9,11},{10,... | collective-permute-start | bytes 393224 | tf_op jit(solution)/shard_map/ppermute | solution.py:239
  178.4 8.2 %collective-permute-start.31 = (bf16[512,128]{1,0:T(8,128)(2,1)S(1)}, bf16[512,128]{1,0:T(8,128)(2,1)S(1)}, u32[]{:S(2)}, u32[]{:S(2)}) collective-permute-start(bf16[512,128]{1,0:T(8,128)(2,1)S(1)} %get-tuple-element.96.piece), channel_id=1, source_target_pairs={{0,4},{1,5},{2,6},{3,7},{4,0},{5,1},{6,2},{7,3},{8,12},{9,13},{10,... | collective-permute-start | bytes 393224 | tf_op jit(solution)/shard_map/ppermute | solution.py:239
  180.2 9.0 %collective-permute-start.33 = (bf16[512,128]{1,0:T(8,128)(2,1)S(1)}, bf16[512,128]{1,0:T(8,128)(2,1)S(1)}, u32[]{:S(2)}, u32[]{:S(2)}) collective-permute-start(bf16[512,128]{1,0:T(8,128)(2,1)S(1)} %get-tuple-element.96.piece), channel_id=1, source_target_pairs={{0,6},{1,7},{2,4},{3,5},{4,2},{5,3},{6,0},{7,1},{8,14},{9,15},{10,... | collective-permute-start | bytes 393224 | tf_op jit(solution)/shard_map/ppermute | solution.py:239
  184.7 5.2 %collective-permute-start.36 = (bf16[512,128]{1,0:T(8,128)(2,1)S(1)}, bf16[512,128]{1,0:T(8,128)(2,1)S(1)}, u32[]{:S(2)}, u32[]{:S(2)}) collective-permute-start(bf16[512,128]{1,0:T(8,128)(2,1)S(1)} %collective-permute-done.35.refs_0_), channel_id=1, source_target_pairs={{0,1},{1,0},{2,3},{3,2},{4,5},{5,4},{6,7},{7,6},{8,9},{9,8},{10,11... | collective-permute-start | bytes 393224 | tf_op jit(solution)/shard_map/ppermute | solution.py:248
  186.6 4.8 %collective-permute-start.32 = (bf16[512,128]{1,0:T(8,128)(2,1)S(1)}, bf16[512,128]{1,0:T(8,128)(2,1)S(1)}, u32[]{:S(2)}, u32[]{:S(2)}) collective-permute-start(bf16[512,128]{1,0:T(8,128)(2,1)S(1)} %collective-permute-done.31.refs_0_), channel_id=1, source_target_pairs={{0,1},{1,0},{2,3},{3,2},{4,5},{5,4},{6,7},{7,6},{8,9},{9,8},{10,11... | collective-permute-start | bytes 393224 | tf_op jit(solution)/shard_map/ppermute | solution.py:248
  192.9 6.4 %collective-permute-start.41 = (bf16[512,128]{1,0:T(8,128)(2,1)S(1)}, bf16[512,128]{1,0:T(8,128)(2,1)S(1)}, u32[]{:S(2)}, u32[]{:S(2)}) collective-permute-start(bf16[512,128]{1,0:T(8,128)(2,1)S(1)} %get-tuple-element.104.refs_3_), channel_id=1, source_target_pairs={{0,2},{1,3},{2,0},{3,1},{4,6},{5,7},{6,4},{7,5},{8,10},{9,11},{10,... | collective-permute-start | bytes 393224 | tf_op jit(solution)/shard_map/ppermute | solution.py:239
  193.0 9.7 %collective-permute-start.37 = (bf16[512,128]{1,0:T(8,128)(2,1)S(1)}, bf16[512,128]{1,0:T(8,128)(2,1)S(1)}, u32[]{:S(2)}, u32[]{:S(2)}) collective-permute-start(bf16[512,128]{1,0:T(8,128)(2,1)S(1)} %get-tuple-element.104.refs_3_), channel_id=1, source_target_pairs={{0,4},{1,5},{2,6},{3,7},{4,0},{5,1},{6,2},{7,3},{8,12},{9,13},{10,... | collective-permute-start | bytes 393224 | tf_op jit(solution)/shard_map/ppermute | solution.py:239
  196.2 9.0 %collective-permute-start.39 = (bf16[512,128]{1,0:T(8,128)(2,1)S(1)}, bf16[512,128]{1,0:T(8,128)(2,1)S(1)}, u32[]{:S(2)}, u32[]{:S(2)}) collective-permute-start(bf16[512,128]{1,0:T(8,128)(2,1)S(1)} %get-tuple-element.104.refs_3_), channel_id=1, source_target_pairs={{0,6},{1,7},{2,4},{3,5},{4,2},{5,3},{6,0},{7,1},{8,14},{9,15},{10,... | collective-permute-start | bytes 393224 | tf_op jit(solution)/shard_map/ppermute | solution.py:239
  199.3 6.7 %collective-permute-start.42 = (bf16[512,128]{1,0:T(8,128)(2,1)S(1)}, bf16[512,128]{1,0:T(8,128)(2,1)S(1)}, u32[]{:S(2)}, u32[]{:S(2)}) collective-permute-start(bf16[512,128]{1,0:T(8,128)(2,1)S(1)} %collective-permute-done.41.refs_5_), channel_id=1, source_target_pairs={{0,1},{1,0},{2,3},{3,2},{4,5},{5,4},{6,7},{7,6},{8,9},{9,8},{10,11... | collective-permute-start | bytes 393224 | tf_op jit(solution)/shard_map/ppermute | solution.py:248
  (23 other events, 301.2 us)
